TPU v7x, 32 devices: a whole 2x2x4 slice. The times are simulated.
32 devices in a mesh: tm: 2 (over core), height: 16 (over z, y, x).
Axes of the slice: x: 2, y: 2, z: 4, core: 2. Of those that a mesh axis runs over, the one named last changes fastest.
Arguments:
- clip: bfloat16 [4, 128, 48, 256], P('tm', 'height'), may hold values from -6 to 6
- teacher: bfloat16 [4, 128, 48, 256], P('tm', 'height'), may hold values from -6 to 6
- kernel_one: bfloat16 [6912, 256], P('height'), may hold values from -0.078125 to 0.078125
- kernel_two: bfloat16 [6912, 256], P('height'), may hold values from -0.078125 to 0.078125
Outputs:
- student: bfloat16 [4, 128, 48, 256], P('tm', 'height')
- grad_one: float32 [6912, 256], P('height')
- grad_two: float32 [6912, 256], P('height')
All inputs are finite; a program needn't handle non-finite values.
Results may differ from a plain program's by a relative error of at most 0.013.
Values may be sent and summed in bfloat16 or wider, within the bound.
No kernel may reach another device: no remote copies, remote signals or barrier semaphores. Data moves between devices by JAX's collectives and lax.ppermute only.
A program may use at most 128 MiB of HBM per device.

v0:
```python
import functools
import math

import jax
import jax.numpy as jnp
from jax import lax
from jax.experimental import pallas as pl
from jax.experimental.pallas import tpu as pltpu
from jax.sharding import PartitionSpec as P


BOTH = ("tm", "height")
BF16 = jnp.bfloat16
F32 = jnp.float32
VMEM_LIMIT = 56 * 1024 * 1024
TAPS = 3


def step_bits(blocks):
    bits = blocks.bit_length() - 1
    assert 1 << bits == blocks and bits >= 4, "height size"
    high = list(range(bits - 1, 1, -1))
    return high + [0, 1], [high[1], high[0]] + high[2:] + [1, 0]


def relative_masks(order):
    return [sum(((r >> k) & 1) << bit for k, bit in enumerate(order)) for r in range(1 << len(order))]


def step_pairs(frames_axis, blocks, step):
    orders = step_bits(blocks)
    return [
        (t * blocks + h, t * blocks + (h ^ (1 << orders[t % 2][step])))
        for t in range(frames_axis)
        for h in range(blocks)
    ]


def shifted(value, axis, by):
    count = lax.axis_size(axis)
    return lax.ppermute(value, axis, [(i, i + by) for i in range(count) if 0 <= i + by < count])


def stepped(value, step):
    return lax.ppermute(value, BOTH, step_pairs(lax.axis_size("tm"), lax.axis_size("height"), step))


def swapped(value, group=1):
    return lax.ppermute(value, "tm", [(t, t ^ group) for t in range(lax.axis_size("tm"))])


def gather_kernel(shard, core):
    half = shard.shape[1] // 2
    steps = lax.axis_size("height").bit_length() - 1
    near = lax.dynamic_slice(shard, (0, core * half), (shard.shape[0], half))[None]
    for step in range(steps - 1):
        near = jnp.concatenate([near, stepped(near, step)], axis=0)
    far = stepped(near, steps - 1)
    return near, far, swapped(near), swapped(far)


def total(first, second):
    return first.astype(F32) + second.astype(F32)


def scatter_grad(keep, send, core):
    frames_axis, blocks = lax.axis_size("tm"), lax.axis_size("height")
    here, came = keep, swapped(send)
    count = blocks
    for step in reversed(range(blocks.bit_length() - 1)):
        count //= 2
        got = stepped(total(here[count:], came[count:]).astype(BF16), step)
        here = total(here[:count], came[:count])
        if count > 4:
            here = here.astype(BF16)
        came = got
    own = total(here[0], came[0])
    group = 2
    while group < frames_axis:
        own = total(own, swapped(own, group))
        group *= 2
    other = swapped(own)
    first = jnp.where(core == 0, own, other)
    second = jnp.where(core == 0, other, own)
    return jnp.concatenate([first, second], axis=1)


def column_shift(value, by):
    width = value.shape[1]
    cols = lax.broadcasted_iota(jnp.int32, value.shape, 1)
    rolled = pltpu.roll(value, by % width, 1)
    return jnp.where((cols < by) if by > 0 else (cols >= width + by), 0.0, rolled)


def chunk_tables(blocks):
    masks = [relative_masks(order) for order in step_bits(blocks)]
    return masks, [[mask.index(g) for g in range(blocks)] for mask in masks]


def weight_copies(parts, whole, sems):
    near, far, near_other, far_other = parts
    count, rows, half = near.shape
    core, place = lax.axis_index("tm") & 1, lax.axis_index("height")
    masks, _ = chunk_tables(2 * count)
    for which, (low, high, side) in enumerate(((near, far, core), (near_other, far_other, 1 - core))):
        lanes = pl.ds(pl.multiple_of(side * half, half), half)
        for r in range(2 * count):
            source = (low if r < count else high).at[r % count]
            owner = place ^ jnp.where(side == 0, masks[0][r], masks[1][r])
            pltpu.make_async_copy(
                source, whole.at[pl.ds(pl.multiple_of(owner * rows, rows), rows), lanes], sems.at[which, owner]
            ).start()


def weight_wait(parts, whole, sems, until, done):
    near = parts[0]
    count, rows, half = near.shape
    while done * rows < until and done < 2 * count:
        for which in range(2):
            pltpu.make_async_copy(
                near.at[0], whole.at[pl.ds(done * rows, rows), pl.ds(which * half, half)], sems.at[which, done]
            ).wait()
        done += 1
    return done


def tap_rows(chans, a, b, c):
    first = ((a * TAPS + b) * TAPS + c) * chans
    return slice(first, first + chans)


def stacked_rows(earlier, current, at, frames, rows):
    held = earlier.shape[0]
    pieces = [earlier[t, rows] if t < held else current[t - held, rows] for t in range(at, at + frames)]
    return jnp.concatenate(pieces, axis=0)


def convolve(slab, parts, weights, sums, sems, forward):
    weight_copies(parts, weights, sems)
    done = 0
    for a in range(TAPS):
        for b in range(TAPS):
            value = slab(a, b)
            rows, width, chans = value.shape
            value = value.reshape(rows * width, chans)
            for c in range(TAPS):
                at = tap_rows(chans, a, b, c)
                done = weight_wait(parts, weights, sems, at.stop, done)
                part = lax.dot_general(
                    value, weights[at, :], (((1,), (0 if forward else 1,)), ((), ())), preferred_element_type=F32
                )
                sums[c] = part if a == b == 0 else sums[c] + part
    moved = [sums[c].reshape(rows, width, chans) for c in range(TAPS)]
    by = 1 if forward else -1
    return column_shift(moved[0], by) + moved[1] + column_shift(moved[2], -by)


def conv_one_kernel(earlier, current, near, far, near_o, far_o, hidden, slope, weights, sums, sems):
    frames, rows, width, chans = hidden.shape
    pre = convolve(
        lambda a, b: stacked_rows(earlier, current, a, frames, slice(b, b + rows)),
        (near, far, near_o, far_o), weights, sums, sems, True,
    ).reshape(frames, rows, width, chans)
    gate = 1.0 / (1.0 + jnp.exp(-pre))
    value = (pre * gate).astype(BF16)
    place = lax.axis_index("height")
    row = lax.broadcasted_iota(jnp.int32, value.shape, 1)
    cut = jnp.logical_or(
        jnp.logical_and(row == 0, place == 0),
        jnp.logical_and(row == rows - 1, place == lax.axis_size("height") - 1),
    )
    hidden[...] = jnp.where(cut, jnp.zeros_like(value), value)
    slope[...] = (gate * (1.0 + pre * (1.0 - gate)))[:, 1 : rows - 1]


def conv_two_kernel(
    factor, earlier, current, clip, teacher, near, far, near_o, far_o, student, dout, weights, sums, sems
):
    frames, rows, width, chans = student.shape
    branch = convolve(
        lambda a, b: stacked_rows(earlier, current, a, frames, slice(b, b + rows)),
        (near, far, near_o, far_o), weights, sums, sems, True,
    ).reshape(frames, rows, width, chans)
    output = clip[...].astype(F32) + branch
    student[...] = output.astype(BF16)
    dout[...] = ((output - teacher[...].astype(F32)) * factor).astype(BF16)


def dpre_kernel(current, later, slope, near, far, near_o, far_o, dpre, weights, sums, sems):
    frames, rows, width, chans = dpre.shape
    back = convolve(
        lambda a, b: stacked_rows(current, later, 2 - a, frames, slice(2 - b, 2 - b + rows)),
        (near, far, near_o, far_o), weights, sums, sems, False,
    ).reshape(frames, rows, width, chans)
    dpre[...] = (back * slope[...]).astype(BF16)


def weight_grad_kernel(margin, earlier, current, grads, keep, send, stage, sems):
    frames, rows, width, chans = grads.shape
    size = frames * rows * width
    near = grads[...].reshape(frames * rows, width, chans)
    wide = near.astype(F32)
    moved = [
        (column_shift(wide, c - 1).astype(BF16) if c != 1 else near).reshape(size, chans) for c in range(TAPS)
    ]
    count, depth, half = keep.shape
    core, place = lax.axis_index("tm") & 1, lax.axis_index("height")
    _, places = chunk_tables(count)
    copies = []
    done = 0
    for a in range(TAPS):
        for b in range(TAPS):
            value = stacked_rows(earlier, current, a, frames, slice(b + margin, b + margin + rows))
            turned = value.reshape(size, chans).T
            for c in range(TAPS):
                at = tap_rows(chans, a, b, c)
                stage[at, :] = jnp.dot(turned, moved[c], preferred_element_type=F32).astype(BF16)
                while (done + 1) * depth <= at.stop and done < count:
                    for which, (to, side) in enumerate(((keep, core), (send, 1 - core))):
                        lanes = pl.ds(pl.multiple_of(side * half, half), half)
                        target = jnp.where(side == 0, places[0][done], places[1][done]) ^ position(place, side)
                        copy = pltpu.make_async_copy(
                            stage.at[pl.ds(done * depth, depth), lanes], to.at[target], sems.at[which, done]
                        )
                        copy.start()
                        copies.append(copy)
                    done += 1
    for copy in copies:
        copy.wait()


def position(place, side):
    blocks = lax.axis_size("height")
    result = 0
    for first, second in zip(*(enumerate_bits(order) for order in step_bits(blocks))):
        bit0 = ((place >> first[1]) & 1) << first[0]
        bit1 = ((place >> second[1]) & 1) << second[0]
        result = result | jnp.where(side == 0, bit0, bit1)
    return result


def enumerate_bits(order):
    return list(enumerate(order))


VM = pl.BlockSpec(memory_space=pltpu.VMEM)
HB = pl.BlockSpec(memory_space=pl.ANY)


def call(kernel, ins, outs, out_shape, scratch):
    return pl.pallas_call(
        kernel,
        in_specs=ins,
        out_specs=outs,
        out_shape=out_shape,
        scratch_shapes=scratch,
        compiler_params=pltpu.CompilerParams(vmem_limit_bytes=VMEM_LIMIT),
    )


def step(clip, teacher, kernel_one, kernel_two):
    frames_n, height_n, width_n, chans = clip.shape
    frames_axis, blocks = lax.axis_size("tm"), lax.axis_size("height")
    assert frames_axis & (frames_axis - 1) == 0 and frames_axis >= 2, "tm size"
    assert frames_n >= 2 and height_n >= 2, "block size"
    depth, half = kernel_one.shape[0], chans // 2
    core = lax.axis_index("tm") & 1

    one = gather_kernel(kernel_one, core)
    two = gather_kernel(kernel_two, core)

    above = shifted(clip[:, height_n - 2 :], "height", 1)
    below = shifted(clip[:, :2], "height", -1)
    clip_ext = jnp.concatenate([above, clip, below], axis=1)
    clip_before = shifted(clip_ext[frames_n - 2 :], "tm", 1)

    weights = pltpu.VMEM((depth * blocks, chans), BF16)
    weight_sems = pltpu.SemaphoreType.DMA((2, blocks))
    block = (frames_n, height_n, width_n, chans)

    def sums(rows):
        return pltpu.VMEM((TAPS, frames_n * rows * width_n, chans), F32)

    hidden, slope = call(
        conv_one_kernel,
        [VM, VM] + [HB] * 4,
        [VM, VM],
        [
            jax.ShapeDtypeStruct((frames_n, height_n + 2, width_n, chans), BF16),
            jax.ShapeDtypeStruct(block, F32),
        ],
        [weights, sums(height_n + 2), weight_sems],
    )(clip_before, clip_ext, *one)

    hidden_before = shifted(hidden[frames_n - 2 :], "tm", 1)
    count_all = frames_n * frames_axis * height_n * blocks * width_n
    student, dout = call(
        functools.partial(conv_two_kernel, 1.0 / math.sqrt(count_all)),
        [VM] * 4 + [HB] * 4,
        [VM, VM],
        [jax.ShapeDtypeStruct(block, BF16)] * 2,
        [weights, sums(height_n), weight_sems],
    )(hidden_before, hidden, clip, teacher, *two)

    d_above = shifted(dout[:, height_n - 1 :], "height", 1)
    d_below = shifted(dout[:, :1], "height", -1)

    grad_shape = jax.ShapeDtypeStruct((blocks, depth, half), BF16)

    def weight_grad(margin, earlier, current, grads):
        return call(
            functools.partial(weight_grad_kernel, margin),
            [VM, VM, VM],
            [HB, HB],
            [grad_shape] * 2,
            [weights, weight_sems],
        )(earlier, current, grads)

    keep_two, send_two = weight_grad(0, hidden_before, hidden, dout)
    grad_two = scatter_grad(keep_two, send_two, core)

    dout_ext = jnp.concatenate([d_above, dout, d_below], axis=1)
    dout_after = shifted(dout_ext[:2], "tm", -1)
    dpre = call(
        dpre_kernel, [VM] * 3 + [HB] * 4, VM, jax.ShapeDtypeStruct(block, BF16), [weights, sums(height_n), weight_sems]
    )(dout_ext, dout_after, slope, *two)
    keep_one, send_one = weight_grad(1, clip_before, clip_ext, dpre)
    grad_one = scatter_grad(keep_one, send_one, core)
    return (student, grad_one, grad_two)


def solution(mesh):
    in_specs = (
        P("tm", "height", None, None),
        P("tm", "height", None, None),
        P("height", None),
        P("height", None),
    )
    out_specs = (P("tm", "height", None, None), P("height", None), P("height", None))
    return jax.shard_map(step, mesh=mesh, in_specs=in_specs, out_specs=out_specs, check_vma=False)
```

profile of v0, /device:TPU:0, one launch (start us, length us, event | category | flops | bytes accessed | tf_op | source)
XLA Modules:
  0.0 180.9 jit_solution(13544852188301228499)
XLA Ops:
  1.6 4.1 %collective-permute-start.3 = (bf16[1,432,128]{2,1,0:T(8,128)(2,1)S(1)}, bf16[1,432,128]{2,1,0:T(8,128)(2,1)S(1)}, u32[]{:S(2)}, u32[]{:S(2)}) collective-permute-start(bf16[1,432,128]{2,1,0:T(8,128)(2,1)S(1)} %dynamic-slice_bitcast_fusion.1), channel_id=1, source_target_pairs={{0,8},{1,9},{2,10},{3,11},{4,12},{5,13},{6,14},{7,15},{8,0},{9,1},... | collective-permute-start | bytes 331784 | tf_op jit(solution)/shard_map/ppermute | solution.py:45
  5.7 2.7 %collective-permute-done.3 = bf16[1,432,128]{2,1,0:T(8,128)(2,1)S(1)} collective-permute-done((bf16[1,432,128]{2,1,0:T(8,128)(2,1)S(1)}, bf16[1,432,128]{2,1,0:T(8,128)(2,1)S(1)}, u32[]{:S(2)}, u32[]{:S(2)}) %collective-permute-start.3) | collective-permute-done | bytes 110624 | tf_op jit(solution)/shard_map/ppermute | solution.py:45
  8.5 2.3 %collective-permute-start.4 = (bf16[2,432,128]{2,1,0:T(8,128)(2,1)S(1)}, bf16[2,432,128]{2,1,0:T(8,128)(2,1)S(1)}, u32[]{:S(2)}, u32[]{:S(2)}) collective-permute-start(bf16[2,432,128]{2,1,0:T(8,128)(2,1)S(1)} %pad_maximum_fusion.6), channel_id=1, source_target_pairs={{0,4},{1,5},{2,6},{3,7},{4,0},{5,1},{6,2},{7,3},{8,12},{9,13},{10,... | collective-permute-start | bytes 663560 | tf_op jit(solution)/shard_map/ppermute | solution.py:45
  11.6 3.4 %collective-permute-start.10 = (bf16[1,432,128]{2,1,0:T(8,128)(2,1)S(1)}, bf16[1,432,128]{2,1,0:T(8,128)(2,1)S(1)}, u32[]{:S(2)}, u32[]{:S(2)}) collective-permute-start(bf16[1,432,128]{2,1,0:T(8,128)(2,1)S(1)} %dynamic-slice_bitcast_fusion), channel_id=1, source_target_pairs={{0,8},{1,9},{2,10},{3,11},{4,12},{5,13},{6,14},{7,15},{8,0},{9,1},... | collective-permute-start | bytes 331784 | tf_op jit(solution)/shard_map/ppermute | solution.py:45
  15.0 3.2 %collective-permute-done.4 = bf16[2,432,128]{2,1,0:T(8,128)(2,1)S(1)} collective-permute-done((bf16[2,432,128]{2,1,0:T(8,128)(2,1)S(1)}, bf16[2,432,128]{2,1,0:T(8,128)(2,1)S(1)}, u32[]{:S(2)}, u32[]{:S(2)}) %collective-permute-start.4) | collective-permute-done | bytes 221216 | tf_op jit(solution)/shard_map/ppermute | solution.py:45
  18.2 1.9 %collective-permute-start.5 = (bf16[4,432,128]{2,1,0:T(8,128)(2,1)S(1)}, bf16[4,432,128]{2,1,0:T(8,128)(2,1)S(1)}, u32[]{:S(2)}, u32[]{:S(2)}) collective-permute-start(bf16[4,432,128]{2,1,0:T(8,128)(2,1)S(1)} %pad_maximum_fusion.2), channel_id=1, source_target_pairs={{0,1},{1,0},{2,3},{3,2},{4,5},{5,4},{6,7},{7,6},{8,9},{9,8},{10,11... | collective-permute-start | bytes 1327112 | tf_op jit(solution)/shard_map/ppermute | solution.py:45
  20.2 6.9 %collective-permute-done.11 = bf16[2,432,128]{2,1,0:T(8,128)(2,1)S(1)} collective-permute-done((bf16[2,432,128]{2,1,0:T(8,128)(2,1)S(1)}, bf16[2,432,128]{2,1,0:T(8,128)(2,1)S(1)}, u32[]{:S(2)}, u32[]{:S(2)}) %collective-permute-start.11) | collective-permute-done | bytes 221216 | tf_op jit(solution)/shard_map/ppermute | solution.py:45
  28.3 2.2 %collective-permute-start.6 = (bf16[8,432,128]{2,1,0:T(8,128)(2,1)S(1)}, bf16[8,432,128]{2,1,0:T(8,128)(2,1)S(1)}, u32[]{:S(2)}, u32[]{:S(2)}) collective-permute-start(bf16[8,432,128]{2,1,0:T(8,128)(2,1)S(1)} %pad_maximum_fusion.near), channel_id=1, source_target_pairs={{0,2},{1,3},{2,0},{3,1},{4,6},{5,7},{6,4},{7,5},{8,10},{9,11},{10,... | collective-permute-start | bytes 2654216 | tf_op jit(solution)/shard_map/ppermute | solution.py:45
  30.5 9.9 %collective-permute-done.12 = bf16[4,432,128]{2,1,0:T(8,128)(2,1)S(1)} collective-permute-done((bf16[4,432,128]{2,1,0:T(8,128)(2,1)S(1)}, bf16[4,432,128]{2,1,0:T(8,128)(2,1)S(1)}, u32[]{:S(2)}, u32[]{:S(2)}) %collective-permute-start.12) | collective-permute-done | bytes 442400 | tf_op jit(solution)/shard_map/ppermute | solution.py:45
  40.4 1.6 collective-permute-start.13
  42.0 3.4 %collective-permute-start = (bf16[2,2,48,256]{3,2,1,0:T(8,128)(2,1)S(1)}, bf16[2,2,48,256]{3,2,1,0:T(8,128)(2,1)S(1)}, u32[]{:S(2)}, u32[]{:S(2)}) collective-permute-start(bf16[2,2,48,256]{3,2,1,0:T(8,128)(2,1)S(1)} %get-tuple-element.38), channel_id=1, source_target_pairs={{0,1},{1,2},{2,3},{3,4},{4,5},{5,6},{6,7},{7,8},{8,9},{9,10},{10,1... | collective-permute-start | bytes 294920 | tf_op jit(solution)/shard_map/ppermute | solution.py:41
  48.6 4.4 %collective-permute-done.1 = bf16[2,2,48,256]{3,2,1,0:T(8,128)(2,1)S(1)} collective-permute-done((bf16[2,2,48,256]{3,2,1,0:T(8,128)(2,1)S(1)}, bf16[2,2,48,256]{3,2,1,0:T(8,128)(2,1)S(1)}, u32[]{:S(2)}, u32[]{:S(2)}) %collective-permute-start.1) | collective-permute-done | bytes 98336 | tf_op jit(solution)/shard_map/ppermute | solution.py:41
  53.0 5.5 %collective-permute-start.2 = (bf16[2,12,48,256]{3,2,1,0:T(8,128)(2,1)S(1)}, bf16[2,12,48,256]{3,2,1,0:T(8,128)(2,1)S(1)}, u32[]{:S(2)}, u32[]{:S(2)}) collective-permute-start(bf16[2,12,48,256]{3,2,1,0:T(8,128)(2,1)S(1)} %constant_dynamic-update-slice_fusion.current), channel_id=1, source_target_pairs={{0,16},{1,17},{2,18},{3,19},{4,20},{5,21},{6,22},{7,23},{8,24},{9,... | collective-permute-start | bytes 1769480 | tf_op jit(solution)/shard_map/ppermute | solution.py:41
  61.2 12.2 %shard_map.67 = (bf16[2,10,48,256]{3,2,1,0:T(8,128)(2,1)}, f32[2,8,48,256]{3,2,1,0:T(8,128)}) custom-call(bf16[2,12,48,256]{3,2,1,0:T(8,128)(2,1)} %copy-done.8, bf16[2,12,48,256]{3,2,1,0:T(8,128)(2,1)} %copy-done.6, bf16[8,432,128]{2,1,0:T(8,128)(2,1)} %copy-done.2, bf16[8,432,128]{2,1,0:T(8,128)(2,1)} %copy-done.12, bf16[8,432,128]{2,1,0:T(8,128)(2,1)} %copy-done.13, ...), custom_call_target="tpu_custom_call" | custom-call | tf_op jit(solution)/shard_map/pallas_call | solution.py:284
  73.5 2.5 %collective-permute-start.9 = (bf16[2,10,48,256]{3,2,1,0:T(8,128)(2,1)}, bf16[2,10,48,256]{3,2,1,0:T(8,128)(2,1)S(1)}, u32[]{:S(2)}, u32[]{:S(2)}) collective-permute-start(bf16[2,10,48,256]{3,2,1,0:T(8,128)(2,1)} %get-tuple-element.11.current), channel_id=1, source_target_pairs={{0,16},{1,17},{2,18},{3,19},{4,20},{5,21},{6,22},{7,23},{8,24},{9,... | collective-permute-start | bytes 1474568 | tf_op jit(solution)/shard_map/ppermute | solution.py:41
  78.2 10.7 %shard_map.68 = (bf16[2,8,48,256]{3,2,1,0:T(8,128)(2,1)}, bf16[2,8,48,256]{3,2,1,0:T(8,128)(2,1)}) custom-call(bf16[2,10,48,256]{3,2,1,0:T(8,128)(2,1)} %copy-done.9, bf16[2,10,48,256]{3,2,1,0:T(8,128)(2,1)} %get-tuple-element.11.current, bf16[2,8,48,256]{3,2,1,0:T(8,128)(2,1)} %clip.1, bf16[2,8,48,256]{3,2,1,0:T(8,128)(2,1)} %teacher.1, ...), custom_call_target="tpu_custom_call" | custom-call | tf_op jit(solution)/shard_map/pallas_call | solution.py:297
  89.8 3.9 %collective-permute-start.16 = (bf16[2,1,48,256]{3,2,1,0:T(8,128)(2,1)S(1)}, bf16[2,1,48,256]{3,2,1,0:T(8,128)(2,1)S(1)}, u32[]{:S(2)}, u32[]{:S(2)}) collective-permute-start(bf16[2,1,48,256]{3,2,1,0:T(8,128)(2,1)S(1)} %get-tuple-element.36), channel_id=1, source_target_pairs={{0,1},{1,2},{2,3},{3,4},{4,5},{5,6},{6,7},{7,8},{8,9},{9,10},{10,1... | collective-permute-start | bytes 147464 | tf_op jit(solution)/shard_map/ppermute | solution.py:41
  96.5 3.2 %collective-permute-done.17 = bf16[2,1,48,256]{3,2,1,0:T(8,128)(2,1)S(1)} collective-permute-done((bf16[2,1,48,256]{3,2,1,0:T(8,128)(2,1)S(1)}, bf16[2,1,48,256]{3,2,1,0:T(8,128)(2,1)S(1)}, u32[]{:S(2)}, u32[]{:S(2)}) %collective-permute-start.17) | collective-permute-done | bytes 49184 | tf_op jit(solution)/shard_map/ppermute | solution.py:41
  101.0 5.3 %shard_map.71 = (bf16[16,432,128]{2,1,0:T(8,128)(2,1)}, bf16[16,432,128]{2,1,0:T(8,128)(2,1)}) custom-call(bf16[2,10,48,256]{3,2,1,0:T(8,128)(2,1)} %copy-done.9, bf16[2,10,48,256]{3,2,1,0:T(8,128)(2,1)} %get-tuple-element.11.current, bf16[2,8,48,256]{3,2,1,0:T(8,128)(2,1)} %get-tuple-element.13.grads), custom_call_target="tpu_custom_call" | custom-call | tf_op jit(solution)/shard_map/pallas_call | solution.py:311
  108.3 11.2 %shard_map.69.grads = bf16[2,8,48,256]{3,2,1,0:T(8,128)(2,1)} custom-call(bf16[2,10,48,256]{3,2,1,0:T(8,128)(2,1)} %copy-done.14, bf16[2,10,48,256]{3,2,1,0:T(8,128)(2,1)} %copy-done.15, f32[2,8,48,256]{3,2,1,0:T(8,128)} %get-tuple-element.14.slope, bf16[8,432,128]{2,1,0:T(8,128)(2,1)} %copy-done.1, bf16[8,432,128]{2,1,0:T(8,128)(2,1)} %copy-done.3, ...), custom_call_target="tpu_custom_call" | custom-call | tf_op jit(solution)/shard_map/pallas_call | solution.py:324
  119.4 5.3 %shard_map.70 = (bf16[16,432,128]{2,1,0:T(8,128)(2,1)}, bf16[16,432,128]{2,1,0:T(8,128)(2,1)}) custom-call(bf16[2,12,48,256]{3,2,1,0:T(8,128)(2,1)} %copy-done.8, bf16[2,12,48,256]{3,2,1,0:T(8,128)(2,1)} %copy-done.6, bf16[2,8,48,256]{3,2,1,0:T(8,128)(2,1)} %shard_map.69.grads), custom_call_target="tpu_custom_call" | custom-call | tf_op jit(solution)/shard_map/pallas_call | solution.py:311
  125.8 3.0 %collective-permute-done.19 = bf16[16,432,128]{2,1,0:T(8,128)(2,1)S(1)} collective-permute-done((bf16[16,432,128]{2,1,0:T(8,128)(2,1)}, bf16[16,432,128]{2,1,0:T(8,128)(2,1)S(1)}, u32[]{:S(2)}, u32[]{:S(2)}) %collective-permute-start.19) | collective-permute-done | bytes 1769504 | tf_op jit(solution)/shard_map/ppermute | solution.py:49
  129.5 9.0 %collective-permute-done.26 = bf16[8,432,128]{2,1,0:T(8,128)(2,1)S(1)} collective-permute-done((bf16[8,432,128]{2,1,0:T(8,128)(2,1)S(1)}, bf16[8,432,128]{2,1,0:T(8,128)(2,1)S(1)}, u32[]{:S(2)}, u32[]{:S(2)}) %collective-permute-start.26) | collective-permute-done | bytes 884768 | tf_op jit(solution)/shard_map/ppermute | solution.py:45
  138.7 1.6 collective-permute-start.27
  140.3 12.4 %collective-permute-done.20 = bf16[8,432,128]{2,1,0:T(8,128)(2,1)S(1)} collective-permute-done((bf16[8,432,128]{2,1,0:T(8,128)(2,1)S(1)}, bf16[8,432,128]{2,1,0:T(8,128)(2,1)S(1)}, u32[]{:S(2)}, u32[]{:S(2)}) %collective-permute-start.20) | collective-permute-done | bytes 884768 | tf_op jit(solution)/shard_map/ppermute | solution.py:45
  152.9 1.6 collective-permute-start.21
  154.8 6.5 %collective-permute-done.21 = bf16[4,432,128]{2,1,0:T(8,128)(2,1)S(1)} collective-permute-done((bf16[4,432,128]{2,1,0:T(8,128)(2,1)S(1)}, bf16[4,432,128]{2,1,0:T(8,128)(2,1)S(1)}, u32[]{:S(2)}, u32[]{:S(2)}) %collective-permute-start.21) | collective-permute-done | bytes 442400 | tf_op jit(solution)/shard_map/ppermute | solution.py:45
  161.4 1.4 collective-permute-done.28
  162.9 2.1 %collective-permute-start.29 = (bf16[1,432,128]{2,1,0:T(8,128)(2,1)S(1)}, bf16[1,432,128]{2,1,0:T(8,128)(2,1)S(1)}, u32[]{:S(2)}, u32[]{:S(2)}) collective-permute-start(bf16[1,432,128]{2,1,0:T(8,128)(2,1)S(1)} %fusion.2), channel_id=1, source_target_pairs={{0,8},{1,9},{2,10},{3,11},{4,12},{5,13},{6,14},{7,15},{8,0},{9,1},... | collective-permute-start | bytes 331784 | tf_op jit(solution)/shard_map/ppermute | solution.py:45
  165.0 6.1 %collective-permute-done.22 = bf16[2,432,128]{2,1,0:T(8,128)(2,1)S(1)} collective-permute-done((bf16[2,432,128]{2,1,0:T(8,128)(2,1)S(1)}, bf16[2,432,128]{2,1,0:T(8,128)(2,1)S(1)}, u32[]{:S(2)}, u32[]{:S(2)}) %collective-permute-start.22) | collective-permute-done | bytes 221216 | tf_op jit(solution)/shard_map/ppermute | solution.py:45
  171.5 6.2 %collective-permute-done.23 = bf16[1,432,128]{2,1,0:T(8,128)(2,1)S(1)} collective-permute-done((bf16[1,432,128]{2,1,0:T(8,128)(2,1)S(1)}, bf16[1,432,128]{2,1,0:T(8,128)(2,1)S(1)}, u32[]{:S(2)}, u32[]{:S(2)}) %collective-permute-start.23) | collective-permute-done | bytes 110624 | tf_op jit(solution)/shard_map/ppermute | solution.py:45
  177.8 1.4 collective-permute-done.24
  (96 shorter events, 22.9 us)
Async XLA Ops:
  1.6 6.9 %collective-permute-start.3 = (bf16[1,432,128]{2,1,0:T(8,128)(2,1)S(1)}, bf16[1,432,128]{2,1,0:T(8,128)(2,1)S(1)}, u32[]{:S(2)}, u32[]{:S(2)}) collective-permute-start(bf16[1,432,128]{2,1,0:T(8,128)(2,1)S(1)} %dynamic-slice_bitcast_fusion.1), channel_id=1, source_target_pairs={{0,8},{1,9},{2,10},{3,11},{4,12},{5,13},{6,14},{7,15},{8,0},{9,1},... | collective-permute-start | bytes 331784 | tf_op jit(solution)/shard_map/ppermute | solution.py:45
  8.5 9.7 %collective-permute-start.4 = (bf16[2,432,128]{2,1,0:T(8,128)(2,1)S(1)}, bf16[2,432,128]{2,1,0:T(8,128)(2,1)S(1)}, u32[]{:S(2)}, u32[]{:S(2)}) collective-permute-start(bf16[2,432,128]{2,1,0:T(8,128)(2,1)S(1)} %pad_maximum_fusion.6), channel_id=1, source_target_pairs={{0,4},{1,5},{2,6},{3,7},{4,0},{5,1},{6,2},{7,3},{8,12},{9,13},{10,... | collective-permute-start | bytes 663560 | tf_op jit(solution)/shard_map/ppermute | solution.py:45
  11.6 8.5 %collective-permute-start.10 = (bf16[1,432,128]{2,1,0:T(8,128)(2,1)S(1)}, bf16[1,432,128]{2,1,0:T(8,128)(2,1)S(1)}, u32[]{:S(2)}, u32[]{:S(2)}) collective-permute-start(bf16[1,432,128]{2,1,0:T(8,128)(2,1)S(1)} %dynamic-slice_bitcast_fusion), channel_id=1, source_target_pairs={{0,8},{1,9},{2,10},{3,11},{4,12},{5,13},{6,14},{7,15},{8,0},{9,1},... | collective-permute-start | bytes 331784 | tf_op jit(solution)/shard_map/ppermute | solution.py:45
  18.2 9.9 %collective-permute-start.5 = (bf16[4,432,128]{2,1,0:T(8,128)(2,1)S(1)}, bf16[4,432,128]{2,1,0:T(8,128)(2,1)S(1)}, u32[]{:S(2)}, u32[]{:S(2)}) collective-permute-start(bf16[4,432,128]{2,1,0:T(8,128)(2,1)S(1)} %pad_maximum_fusion.2), channel_id=1, source_target_pairs={{0,1},{1,0},{2,3},{3,2},{4,5},{5,4},{6,7},{7,6},{8,9},{9,8},{10,11... | collective-permute-start | bytes 1327112 | tf_op jit(solution)/shard_map/ppermute | solution.py:45
  20.2 7.0 %collective-permute-start.11 = (bf16[2,432,128]{2,1,0:T(8,128)(2,1)S(1)}, bf16[2,432,128]{2,1,0:T(8,128)(2,1)S(1)}, u32[]{:S(2)}, u32[]{:S(2)}) collective-permute-start(bf16[2,432,128]{2,1,0:T(8,128)(2,1)S(1)} %pad_maximum_fusion.7), channel_id=1, source_target_pairs={{0,4},{1,5},{2,6},{3,7},{4,0},{5,1},{6,2},{7,3},{8,12},{9,13},{10,... | collective-permute-start | bytes 663560 | tf_op jit(solution)/shard_map/ppermute | solution.py:45
  27.2 13.1 %collective-permute-start.12 = (bf16[4,432,128]{2,1,0:T(8,128)(2,1)S(1)}, bf16[4,432,128]{2,1,0:T(8,128)(2,1)S(1)}, u32[]{:S(2)}, u32[]{:S(2)}) collective-permute-start(bf16[4,432,128]{2,1,0:T(8,128)(2,1)S(1)} %pad_maximum_fusion.3), channel_id=1, source_target_pairs={{0,1},{1,0},{2,3},{3,2},{4,5},{5,4},{6,7},{7,6},{8,9},{9,8},{10,11... | collective-permute-start | bytes 1327112 | tf_op jit(solution)/shard_map/ppermute | solution.py:45
  28.3 18.5 %collective-permute-start.6 = (bf16[8,432,128]{2,1,0:T(8,128)(2,1)S(1)}, bf16[8,432,128]{2,1,0:T(8,128)(2,1)S(1)}, u32[]{:S(2)}, u32[]{:S(2)}) collective-permute-start(bf16[8,432,128]{2,1,0:T(8,128)(2,1)S(1)} %pad_maximum_fusion.near), channel_id=1, source_target_pairs={{0,2},{1,3},{2,0},{3,1},{4,6},{5,7},{6,4},{7,5},{8,10},{9,11},{10,... | collective-permute-start | bytes 2654216 | tf_op jit(solution)/shard_map/ppermute | solution.py:45
  40.4 33.0 %copy-start.1 = (bf16[8,432,128]{2,1,0:T(8,128)(2,1)}, bf16[8,432,128]{2,1,0:T(8,128)(2,1)S(1)}, u32[]{:S(2)}) copy-start(bf16[8,432,128]{2,1,0:T(8,128)(2,1)S(1)} %pad_maximum_fusion.1.near) | copy-start | bytes 2654212
  40.4 18.2 %collective-permute-start.13 = (bf16[8,432,128]{2,1,0:T(8,128)(2,1)S(1)}, bf16[8,432,128]{2,1,0:T(8,128)(2,1)S(1)}, u32[]{:S(2)}, u32[]{:S(2)}) collective-permute-start(bf16[8,432,128]{2,1,0:T(8,128)(2,1)S(1)} %pad_maximum_fusion.1.near), channel_id=1, source_target_pairs={{0,2},{1,3},{2,0},{3,1},{4,6},{5,7},{6,4},{7,5},{8,10},{9,11},{10,... | collective-permute-start | bytes 2654216 | tf_op jit(solution)/shard_map/ppermute | solution.py:45
  42.0 6.6 %collective-permute-start = (bf16[2,2,48,256]{3,2,1,0:T(8,128)(2,1)S(1)}, bf16[2,2,48,256]{3,2,1,0:T(8,128)(2,1)S(1)}, u32[]{:S(2)}, u32[]{:S(2)}) collective-permute-start(bf16[2,2,48,256]{3,2,1,0:T(8,128)(2,1)S(1)} %get-tuple-element.38), channel_id=1, source_target_pairs={{0,1},{1,2},{2,3},{3,4},{4,5},{5,6},{6,7},{7,8},{8,9},{9,10},{10,1... | collective-permute-start | bytes 294920 | tf_op jit(solution)/shard_map/ppermute | solution.py:41
  45.4 7.6 %collective-permute-start.1 = (bf16[2,2,48,256]{3,2,1,0:T(8,128)(2,1)S(1)}, bf16[2,2,48,256]{3,2,1,0:T(8,128)(2,1)S(1)}, u32[]{:S(2)}, u32[]{:S(2)}) collective-permute-start(bf16[2,2,48,256]{3,2,1,0:T(8,128)(2,1)S(1)} %get-tuple-element.37), channel_id=1, source_target_pairs={{1,0},{2,1},{3,2},{4,3},{5,4},{6,5},{7,6},{8,7},{9,8},{10,9},{11,1... | collective-permute-start | bytes 294920 | tf_op jit(solution)/shard_map/ppermute | solution.py:41
  46.7 13.4 %collective-permute-start.7 = (bf16[8,432,128]{2,1,0:T(8,128)(2,1)S(1)}, bf16[8,432,128]{2,1,0:T(8,128)(2,1)S(1)}, u32[]{:S(2)}, u32[]{:S(2)}) collective-permute-start(bf16[8,432,128]{2,1,0:T(8,128)(2,1)S(1)} %pad_maximum_fusion.near), channel_id=1, source_target_pairs={{0,16},{16,0},{1,17},{17,1},{2,18},{18,2},{3,19},{19,3},{4,20},{20... | collective-permute-start | bytes 2654216 | tf_op jit(solution)/shard_map/ppermute | solution.py:49
  46.8 13.3 %collective-permute-start.8 = (bf16[8,432,128]{2,1,0:T(8,128)(2,1)S(1)}, bf16[8,432,128]{2,1,0:T(8,128)(2,1)}, u32[]{:S(2)}, u32[]{:S(2)}) collective-permute-start(bf16[8,432,128]{2,1,0:T(8,128)(2,1)S(1)} %collective-permute-done.6.far), channel_id=1, source_target_pairs={{0,16},{16,0},{1,17},{17,1},{2,18},{18,2},{3,19},{19,3},{4,20},{20... | collective-permute-start | bytes 2654216 | tf_op jit(solution)/shard_map/ppermute | solution.py:49
  53.0 7.1 %collective-permute-start.2 = (bf16[2,12,48,256]{3,2,1,0:T(8,128)(2,1)S(1)}, bf16[2,12,48,256]{3,2,1,0:T(8,128)(2,1)S(1)}, u32[]{:S(2)}, u32[]{:S(2)}) collective-permute-start(bf16[2,12,48,256]{3,2,1,0:T(8,128)(2,1)S(1)} %constant_dynamic-update-slice_fusion.current), channel_id=1, source_target_pairs={{0,16},{1,17},{2,18},{3,19},{4,20},{5,21},{6,22},{7,23},{8,24},{9,... | collective-permute-start | bytes 1769480 | tf_op jit(solution)/shard_map/ppermute | solution.py:41
  58.5 17.4 %collective-permute-start.14 = (bf16[8,432,128]{2,1,0:T(8,128)(2,1)S(1)}, bf16[8,432,128]{2,1,0:T(8,128)(2,1)S(1)}, u32[]{:S(2)}, u32[]{:S(2)}) collective-permute-start(bf16[8,432,128]{2,1,0:T(8,128)(2,1)S(1)} %pad_maximum_fusion.1.near), channel_id=1, source_target_pairs={{0,16},{16,0},{1,17},{17,1},{2,18},{18,2},{3,19},{19,3},{4,20},{20... | collective-permute-start | bytes 2654216 | tf_op jit(solution)/shard_map/ppermute | solution.py:49
  58.6 17.4 %collective-permute-start.15 = (bf16[8,432,128]{2,1,0:T(8,128)(2,1)S(1)}, bf16[8,432,128]{2,1,0:T(8,128)(2,1)S(1)}, u32[]{:S(2)}, u32[]{:S(2)}) collective-permute-start(bf16[8,432,128]{2,1,0:T(8,128)(2,1)S(1)} %collective-permute-done.13.far), channel_id=1, source_target_pairs={{0,16},{16,0},{1,17},{17,1},{2,18},{18,2},{3,19},{19,3},{4,20},{20... | collective-permute-start | bytes 2654216 | tf_op jit(solution)/shard_map/ppermute | solution.py:49
  73.5 4.0 %collective-permute-start.9 = (bf16[2,10,48,256]{3,2,1,0:T(8,128)(2,1)}, bf16[2,10,48,256]{3,2,1,0:T(8,128)(2,1)S(1)}, u32[]{:S(2)}, u32[]{:S(2)}) collective-permute-start(bf16[2,10,48,256]{3,2,1,0:T(8,128)(2,1)} %get-tuple-element.11.current), channel_id=1, source_target_pairs={{0,16},{1,17},{2,18},{3,19},{4,20},{5,21},{6,22},{7,23},{8,24},{9,... | collective-permute-start | bytes 1474568 | tf_op jit(solution)/shard_map/ppermute | solution.py:41
  89.8 5.6 %collective-permute-start.16 = (bf16[2,1,48,256]{3,2,1,0:T(8,128)(2,1)S(1)}, bf16[2,1,48,256]{3,2,1,0:T(8,128)(2,1)S(1)}, u32[]{:S(2)}, u32[]{:S(2)}) collective-permute-start(bf16[2,1,48,256]{3,2,1,0:T(8,128)(2,1)S(1)} %get-tuple-element.36), channel_id=1, source_target_pairs={{0,1},{1,2},{2,3},{3,4},{4,5},{5,6},{6,7},{7,8},{8,9},{9,10},{10,1... | collective-permute-start | bytes 147464 | tf_op jit(solution)/shard_map/ppermute | solution.py:41
  93.7 6.0 %collective-permute-start.17 = (bf16[2,1,48,256]{3,2,1,0:T(8,128)(2,1)S(1)}, bf16[2,1,48,256]{3,2,1,0:T(8,128)(2,1)S(1)}, u32[]{:S(2)}, u32[]{:S(2)}) collective-permute-start(bf16[2,1,48,256]{3,2,1,0:T(8,128)(2,1)S(1)} %get-tuple-element.35), channel_id=1, source_target_pairs={{1,0},{2,1},{3,2},{4,3},{5,4},{6,5},{7,6},{8,7},{9,8},{10,9},{11,1... | collective-permute-start | bytes 147464 | tf_op jit(solution)/shard_map/ppermute | solution.py:41
  99.7 7.8 %collective-permute-start.18 = (bf16[2,10,48,256]{3,2,1,0:T(8,128)(2,1)S(1)}, bf16[2,10,48,256]{3,2,1,0:T(8,128)(2,1)S(1)}, u32[]{:S(2)}, u32[]{:S(2)}) collective-permute-start(bf16[2,10,48,256]{3,2,1,0:T(8,128)(2,1)S(1)} %constant_dynamic-update-slice_fusion.3.current), channel_id=1, source_target_pairs={{16,0},{17,1},{18,2},{19,3},{20,4},{21,5},{22,6},{23,7},{24,8},{25... | collective-permute-start | bytes 1474568 | tf_op jit(solution)/shard_map/ppermute | solution.py:41
  106.3 18.6 %collective-permute-start.25 = (bf16[16,432,128]{2,1,0:T(8,128)(2,1)}, bf16[16,432,128]{2,1,0:T(8,128)(2,1)S(1)}, u32[]{:S(2)}, u32[]{:S(2)}) collective-permute-start(bf16[16,432,128]{2,1,0:T(8,128)(2,1)} %get-tuple-element.18), channel_id=1, source_target_pairs={{0,16},{16,0},{1,17},{17,1},{2,18},{18,2},{3,19},{19,3},{4,20},{20... | collective-permute-start | bytes 5308424 | tf_op jit(solution)/shard_map/ppermute | solution.py:49
  124.8 4.0 %collective-permute-start.19 = (bf16[16,432,128]{2,1,0:T(8,128)(2,1)}, bf16[16,432,128]{2,1,0:T(8,128)(2,1)S(1)}, u32[]{:S(2)}, u32[]{:S(2)}) collective-permute-start(bf16[16,432,128]{2,1,0:T(8,128)(2,1)} %get-tuple-element.16), channel_id=1, source_target_pairs={{0,16},{16,0},{1,17},{17,1},{2,18},{18,2},{3,19},{19,3},{4,20},{20... | collective-permute-start | bytes 5308424 | tf_op jit(solution)/shard_map/ppermute | solution.py:49
  125.4 13.1 %collective-permute-start.26 = (bf16[8,432,128]{2,1,0:T(8,128)(2,1)S(1)}, bf16[8,432,128]{2,1,0:T(8,128)(2,1)S(1)}, u32[]{:S(2)}, u32[]{:S(2)}) collective-permute-start(bf16[8,432,128]{2,1,0:T(8,128)(2,1)S(1)} %get-tuple-element.20), channel_id=1, source_target_pairs={{0,2},{1,3},{2,0},{3,1},{4,6},{5,7},{6,4},{7,5},{8,10},{9,11},{10,... | collective-permute-start | bytes 2654216 | tf_op jit(solution)/shard_map/ppermute | solution.py:45
  129.2 23.5 %collective-permute-start.20 = (bf16[8,432,128]{2,1,0:T(8,128)(2,1)S(1)}, bf16[8,432,128]{2,1,0:T(8,128)(2,1)S(1)}, u32[]{:S(2)}, u32[]{:S(2)}) collective-permute-start(bf16[8,432,128]{2,1,0:T(8,128)(2,1)S(1)} %get-tuple-element.22), channel_id=1, source_target_pairs={{0,2},{1,3},{2,0},{3,1},{4,6},{5,7},{6,4},{7,5},{8,10},{9,11},{10,... | collective-permute-start | bytes 2654216 | tf_op jit(solution)/shard_map/ppermute | solution.py:45
  138.7 15.9 %collective-permute-start.27 = (bf16[4,432,128]{2,1,0:T(8,128)(2,1)S(1)}, bf16[4,432,128]{2,1,0:T(8,128)(2,1)S(1)}, u32[]{:S(2)}, u32[]{:S(2)}) collective-permute-start(bf16[4,432,128]{2,1,0:T(8,128)(2,1)S(1)} %get-tuple-element.23), channel_id=1, source_target_pairs={{0,1},{1,0},{2,3},{3,2},{4,5},{5,4},{6,7},{7,6},{8,9},{9,8},{10,11... | collective-permute-start | bytes 1327112 | tf_op jit(solution)/shard_map/ppermute | solution.py:45
  152.9 8.4 %collective-permute-start.21 = (bf16[4,432,128]{2,1,0:T(8,128)(2,1)S(1)}, bf16[4,432,128]{2,1,0:T(8,128)(2,1)S(1)}, u32[]{:S(2)}, u32[]{:S(2)}) collective-permute-start(bf16[4,432,128]{2,1,0:T(8,128)(2,1)S(1)} %get-tuple-element.25), channel_id=1, source_target_pairs={{0,1},{1,0},{2,3},{3,2},{4,5},{5,4},{6,7},{7,6},{8,9},{9,8},{10,11... | collective-permute-start | bytes 1327112 | tf_op jit(solution)/shard_map/ppermute | solution.py:45
  154.6 8.2 %collective-permute-start.28 = (bf16[2,432,128]{2,1,0:T(8,128)(2,1)S(1)}, bf16[2,432,128]{2,1,0:T(8,128)(2,1)S(1)}, u32[]{:S(2)}, u32[]{:S(2)}) collective-permute-start(bf16[2,432,128]{2,1,0:T(8,128)(2,1)S(1)} %get-tuple-element.27), channel_id=1, source_target_pairs={{0,4},{1,5},{2,6},{3,7},{4,0},{5,1},{6,2},{7,3},{8,12},{9,13},{10,... | collective-permute-start | bytes 663560 | tf_op jit(solution)/shard_map/ppermute | solution.py:45
  161.4 9.7 %collective-permute-start.22 = (bf16[2,432,128]{2,1,0:T(8,128)(2,1)S(1)}, bf16[2,432,128]{2,1,0:T(8,128)(2,1)S(1)}, u32[]{:S(2)}, u32[]{:S(2)}) collective-permute-start(bf16[2,432,128]{2,1,0:T(8,128)(2,1)S(1)} %get-tuple-element.29), channel_id=1, source_target_pairs={{0,4},{1,5},{2,6},{3,7},{4,0},{5,1},{6,2},{7,3},{8,12},{9,13},{10,... | collective-permute-start | bytes 663560 | tf_op jit(solution)/shard_map/ppermute | solution.py:45
  162.9 8.5 %collective-permute-start.29 = (bf16[1,432,128]{2,1,0:T(8,128)(2,1)S(1)}, bf16[1,432,128]{2,1,0:T(8,128)(2,1)S(1)}, u32[]{:S(2)}, u32[]{:S(2)}) collective-permute-start(bf16[1,432,128]{2,1,0:T(8,128)(2,1)S(1)} %fusion.2), channel_id=1, source_target_pairs={{0,8},{1,9},{2,10},{3,11},{4,12},{5,13},{6,14},{7,15},{8,0},{9,1},... | collective-permute-start | bytes 331784 | tf_op jit(solution)/shard_map/ppermute | solution.py:45
  171.1 6.6 %collective-permute-start.23 = (bf16[1,432,128]{2,1,0:T(8,128)(2,1)S(1)}, bf16[1,432,128]{2,1,0:T(8,128)(2,1)S(1)}, u32[]{:S(2)}, u32[]{:S(2)}) collective-permute-start(bf16[1,432,128]{2,1,0:T(8,128)(2,1)S(1)} %fusion.5), channel_id=1, source_target_pairs={{0,8},{1,9},{2,10},{3,11},{4,12},{5,13},{6,14},{7,15},{8,0},{9,1},... | collective-permute-start | bytes 331784 | tf_op jit(solution)/shard_map/ppermute | solution.py:45
  171.4 6.4 %collective-permute-start.30 = (f32[432,128]{1,0:T(8,128)S(1)}, f32[432,128]{1,0:T(8,128)S(1)}, u32[]{:S(2)}, u32[]{:S(2)}) collective-permute-start(f32[432,128]{1,0:T(8,128)S(1)} %fusion.4), channel_id=1, source_target_pairs={{0,16},{16,0},{1,17},{17,1},{2,18},{18,2},{3,19},{19,3},{4,20},{20... | collective-permute-start | bytes 663560 | tf_op jit(solution)/shard_map/ppermute | solution.py:49
  177.7 1.5 collective-permute-start.24
  (15 other events, 117.6 us)
where the time goes:
time: 181 us
  waiting for transfers between devices  80.4 us (44%)
  Pallas kernels  44.7 us (25%)
  starting transfers between devices  44.6 us (25%)
  local copies, waits for them, and re-layouts  6.48 us (4%)
  other arithmetic  3.57 us (2%)
    ppermute x16, waiting for transfers between devices, stepped(): lax.ppermute(value, BOTH, step_pairs(lax.axis_size('tm'), lax.axis_size('...  64.3 us
    ppermute x16, starting transfers between devices, stepped(): lax.ppermute(value, BOTH, step_pairs(lax.axis_size('tm'), lax.axis_size('...  22.9 us
    ppermute x7, starting transfers between devices, shifted(): lax.ppermute(value, axis, [(i, i + by) for i in range(count) if 0 <= i +...  19.1 us
    pallas_call x1, Pallas kernels, step(): call(conv_one_kernel, [VM, VM] + [HB] * 4, [VM, VM], [jax.ShapeDtypeStruc...  12.2 us
    ppermute x7, waiting for transfers between devices, shifted(): lax.ppermute(value, axis, [(i, i + by) for i in range(count) if 0 <= i +...  11.7 us
    pallas_call x1, Pallas kernels, step(): call(dpre_kernel, [VM] * 3 + [HB] * 4, VM, jax.ShapeDtypeStruct(block, BF...  11.2 us
    pallas_call x1, Pallas kernels, step(): call(functools.partial(conv_two_kernel, 1.0 / math.sqrt(count_all)), [VM]...  10.7 us
    pallas_call x2, Pallas kernels, weight_grad(): call(functools.partial(weight_grad_kernel, margin), [VM, VM, VM], [HB, HB...  10.6 us
  transfers between devices with their start and end apart: 31, of which 18 were waited for; matrix products, arithmetic and copies ran while one was open for 2% of the time, Pallas kernels for 19%

commit v1 on v0

v1 whole, which is shorter than its diff:
```python
import functools
import math

import jax
import jax.numpy as jnp
from jax import lax
from jax.experimental import pallas as pl
from jax.experimental.pallas import tpu as pltpu
from jax.sharding import PartitionSpec as P


BOTH = ("tm", "height")
BF16 = jnp.bfloat16
F32 = jnp.float32
VMEM_LIMIT = 24 * 1024 * 1024
TAPS = 3


def step_bits(blocks, late):
    bits = blocks.bit_length() - 1
    assert 1 << bits == blocks and bits >= 4, "height size"
    high = list(range(bits - 1, 1, -1))
    swap = [high[1], high[0]] + high[2:]
    if late:
        return high + [0, 1], swap + [1, 0]
    return [0] + high + [1], [1] + swap + [0]


def relative_masks(order):
    return [sum(((r >> k) & 1) << bit for k, bit in enumerate(order)) for r in range(1 << len(order))]


def step_pairs(frames_axis, blocks, step, late):
    orders = step_bits(blocks, late)
    return [
        (t * blocks + h, t * blocks + (h ^ (1 << orders[t % 2][step])))
        for t in range(frames_axis)
        for h in range(blocks)
    ]


def shifted(value, axis, by):
    count = lax.axis_size(axis)
    return lax.ppermute(value, axis, [(i, i + by) for i in range(count) if 0 <= i + by < count])


def stepped(value, step, late):
    return lax.ppermute(value, BOTH, step_pairs(lax.axis_size("tm"), lax.axis_size("height"), step, late))


def swapped(value, group=1):
    return lax.ppermute(value, "tm", [(t, t ^ group) for t in range(lax.axis_size("tm"))])


def gather_kernel(shard, core, late):
    half = shard.shape[1] // 2
    steps = lax.axis_size("height").bit_length() - 1
    near = lax.dynamic_slice(shard, (0, core * half), (shard.shape[0], half))[None]
    for step in range(steps - 1):
        near = jnp.concatenate([near, stepped(near, step, late)], axis=0)
    far = stepped(near, steps - 1, late)
    return near, far, swapped(near), swapped(far)


def total(first, second):
    return first.astype(F32) + second.astype(F32)


def scatter_grad(keep, send, core, late):
    frames_axis, blocks = lax.axis_size("tm"), lax.axis_size("height")
    here, came = keep, swapped(send)
    count = blocks
    for step in reversed(range(blocks.bit_length() - 1)):
        count //= 2
        got = stepped(total(here[count:], came[count:]).astype(BF16), step, late)
        here = total(here[:count], came[:count])
        if count > 4:
            here = here.astype(BF16)
        came = got
    own = total(here[0], came[0])
    group = 2
    while group < frames_axis:
        own = total(own, swapped(own, group))
        group *= 2
    other = swapped(own)
    first = jnp.where(core == 0, own, other)
    second = jnp.where(core == 0, other, own)
    return jnp.concatenate([first, second], axis=1)


def column_shift(value, by):
    width = value.shape[1]
    cols = lax.broadcasted_iota(jnp.int32, value.shape, 1)
    rolled = pltpu.roll(value, by % width, 1)
    return jnp.where((cols < by) if by > 0 else (cols >= width + by), 0.0, rolled)


def chunk_tables(blocks, late):
    masks = [relative_masks(order) for order in step_bits(blocks, late)]
    return masks, [[mask.index(g) for g in range(blocks)] for mask in masks]


def weight_copies(parts, whole, sems, late):
    near, far, near_other, far_other = parts
    count, rows, half = near.shape
    core, place = lax.axis_index("tm") & 1, lax.axis_index("height")
    masks, _ = chunk_tables(2 * count, late)
    for which, (low, high, side) in enumerate(((near, far, core), (near_other, far_other, 1 - core))):
        lanes = pl.ds(pl.multiple_of(side * half, half), half)
        for r in range(2 * count):
            source = (low if r < count else high).at[r % count]
            owner = place ^ jnp.where(side == 0, masks[0][r], masks[1][r])
            pltpu.make_async_copy(
                source, whole.at[pl.ds(pl.multiple_of(owner * rows, rows), rows), lanes], sems.at[which, owner]
            ).start()


def weight_wait(parts, whole, sems, until, done):
    near = parts[0]
    count, rows, half = near.shape
    while done * rows < until and done < 2 * count:
        for which in range(2):
            pltpu.make_async_copy(
                near.at[0], whole.at[pl.ds(done * rows, rows), pl.ds(which * half, half)], sems.at[which, done]
            ).wait()
        done += 1
    return done


def tap_rows(chans, a, b, c):
    first = ((a * TAPS + b) * TAPS + c) * chans
    return slice(first, first + chans)


def stacked_rows(earlier, current, at, frames, rows):
    held = earlier.shape[0]
    pieces = [earlier[t, rows] if t < held else current[t - held, rows] for t in range(at, at + frames)]
    return jnp.concatenate(pieces, axis=0)


def convolve(slab, parts, weights, sems, forward, late):
    weight_copies(parts, weights, sems, late)
    order = [(a, b) for a in range(TAPS) for b in range(TAPS)]
    pieces = [slab(a, b) for a, b in order]
    rows, width, chans = pieces[0].shape
    left = jnp.concatenate([piece.reshape(rows * width, chans) for piece in pieces], axis=1)
    weight_wait(parts, weights, sems, weights.shape[0], 0)
    result = None
    for c in range(TAPS):
        blocks = [weights[tap_rows(chans, a, b, c), :] for a, b in order]
        right = jnp.concatenate(blocks, axis=0 if forward else 1)
        part = lax.dot_general(
            left, right, (((1,), (0 if forward else 1,)), ((), ())), preferred_element_type=F32
        ).reshape(rows, width, chans)
        by = (1 - c) if forward else (c - 1)
        if by:
            part = column_shift(part, by)
        result = part if result is None else result + part
    return result


def outside(shape, margin):
    place = lax.axis_index("height")
    row = lax.broadcasted_iota(jnp.int32, shape, 1)
    first = jnp.where(place == 0, margin, 0)
    stop = jnp.where(place == lax.axis_size("height") - 1, shape[1] - margin, shape[1])
    return jnp.logical_or(row < first, row >= stop)


def conv_one_kernel(late, earlier, current, near, far, near_o, far_o, hidden, slope, weights, sems):
    frames, rows, width, chans = hidden.shape
    margin = (rows - slope.shape[1]) // 2
    pre = convolve(
        lambda a, b: stacked_rows(earlier, current, a, frames, slice(b, b + rows)),
        (near, far, near_o, far_o), weights, sems, True, late,
    ).reshape(frames, rows, width, chans)
    gate = 1.0 / (1.0 + jnp.exp(-pre))
    value = (pre * gate).astype(BF16)
    hidden[...] = jnp.where(outside(value.shape, margin), jnp.zeros_like(value), value)
    inner = slice(margin, rows - margin)
    gate, pre = gate[:, inner], pre[:, inner]
    slope[...] = gate * (1.0 + pre * (1.0 - gate))


def conv_two_kernel(
    factor, late, earlier, current, clip, teacher, near, far, near_o, far_o, student, dout, weights, sems
):
    frames, rows, width, chans = dout.shape
    margin = (rows - student.shape[1]) // 2
    skip = (clip.shape[1] - rows) // 2
    branch = convolve(
        lambda a, b: stacked_rows(earlier, current, a, frames, slice(b, b + rows)),
        (near, far, near_o, far_o), weights, sems, True, late,
    ).reshape(frames, rows, width, chans)
    output = clip[:, skip : skip + rows].astype(F32) + branch
    student[...] = output[:, margin : rows - margin].astype(BF16)
    value = ((output - teacher[...].astype(F32)) * factor).astype(BF16)
    dout[...] = jnp.where(outside(value.shape, margin), jnp.zeros_like(value), value)


def dpre_kernel(late, current, later, slope, near, far, near_o, far_o, dpre, weights, sems):
    frames, rows, width, chans = dpre.shape
    back = convolve(
        lambda a, b: stacked_rows(current, later, 2 - a, frames, slice(2 - b, 2 - b + rows)),
        (near, far, near_o, far_o), weights, sems, False, late,
    ).reshape(frames, rows, width, chans)
    dpre[...] = (back * slope[...]).astype(BF16)


def weight_grad_kernel(late, inner, earlier, current, grads, keep, send):
    frames, rows, width, chans = grads.shape
    rows -= 2 * inner
    count, depth, half = keep.shape
    margin = (current.shape[1] - rows) // 2
    size = frames * rows * width
    near = grads[:, inner : inner + rows].reshape(frames * rows, width, chans)
    wide = near.astype(F32)
    moved = [
        (column_shift(wide, c - 1).astype(BF16) if c != 1 else near).reshape(size, chans) for c in range(TAPS)
    ]
    core, place = lax.axis_index("tm") & 1, lax.axis_index("height")
    _, places = chunk_tables(count, late)
    base = [position(place, side, late) for side in (core, 1 - core)]
    for a in range(TAPS):
        for b in range(TAPS):
            first = b + margin - 1
            value = stacked_rows(earlier, current, a, frames, slice(first, first + rows))
            turned = value.reshape(size, chans).T
            for c in range(TAPS):
                at = tap_rows(chans, a, b, c)
                part = jnp.dot(turned, moved[c], preferred_element_type=F32).astype(BF16)
                left, right = part[:, :half], part[:, half:]
                mine = jnp.where(core == 0, left, right)
                theirs = jnp.where(core == 0, right, left)
                start = at.start
                while start < at.stop:
                    chunk = start // depth
                    stop = min(at.stop, (chunk + 1) * depth)
                    here = slice(start - chunk * depth, stop - chunk * depth)
                    there = slice(start - at.start, stop - at.start)
                    for to, block, side, shift in ((keep, mine, core, base[0]), (send, theirs, 1 - core, base[1])):
                        target = jnp.where(side == 0, places[0][chunk], places[1][chunk]) ^ shift
                        to[target, here, :] = block[there]
                    start = stop


def position(place, side, late):
    result = 0
    for k, (bit0, bit1) in enumerate(zip(*step_bits(lax.axis_size("height"), late))):
        result = result | jnp.where(side == 0, ((place >> bit0) & 1) << k, ((place >> bit1) & 1) << k)
    return result


VM = pl.BlockSpec(memory_space=pltpu.VMEM)
HB = pl.BlockSpec(memory_space=pl.ANY)


def call(kernel, ins, outs, out_shape, scratch):
    return pl.pallas_call(
        kernel,
        in_specs=ins,
        out_specs=outs,
        out_shape=out_shape,
        scratch_shapes=scratch,
        compiler_params=pltpu.CompilerParams(vmem_limit_bytes=VMEM_LIMIT),
    )


def step(clip, teacher, kernel_one, kernel_two):
    frames_n, height_n, width_n, chans = clip.shape
    frames_axis, blocks = lax.axis_size("tm"), lax.axis_size("height")
    assert frames_axis & (frames_axis - 1) == 0 and frames_axis >= 2, "tm size"
    assert frames_n >= 2 and height_n >= 3, "block size"
    depth, half = kernel_one.shape[0], chans // 2
    core = lax.axis_index("tm") & 1

    one = gather_kernel(kernel_one, core, True)
    two = gather_kernel(kernel_two, core, False)

    last_rows = jnp.concatenate([clip[:, height_n - 3 :], teacher[:, height_n - 1 :]], axis=1)
    first_rows = jnp.concatenate([clip[:, :3], teacher[:, :1]], axis=1)
    above = shifted(last_rows, "height", 1)
    below = shifted(first_rows, "height", -1)
    clip_ext = jnp.concatenate([above[:, :3], clip, below[:, :3]], axis=1)
    teacher_ext = jnp.concatenate([above[:, 3:], teacher, below[:, 3:]], axis=1)
    clip_before = shifted(clip_ext[frames_n - 2 :], "tm", 1)

    weights = pltpu.VMEM((depth * blocks, chans), BF16)
    scratch = [weights, pltpu.SemaphoreType.DMA((2, blocks))]

    def block(margin, kind=BF16):
        return jax.ShapeDtypeStruct((frames_n, height_n + 2 * margin, width_n, chans), kind)

    hidden, slope = call(
        functools.partial(conv_one_kernel, True), [VM, VM] + [HB] * 4, [VM, VM], [block(2), block(0, F32)], scratch
    )(clip_before, clip_ext, *one)

    hidden_before = shifted(hidden[frames_n - 2 :], "tm", 1)
    count_all = frames_n * frames_axis * height_n * blocks * width_n
    student, dout = call(
        functools.partial(conv_two_kernel, 1.0 / math.sqrt(count_all), False),
        [VM] * 4 + [HB] * 4, [VM, VM], [block(0), block(1)], scratch,
    )(hidden_before, hidden, clip_ext, teacher_ext, *two)

    dout_after = shifted(dout[:2], "tm", -1)

    grad_shape = jax.ShapeDtypeStruct((blocks, depth, half), BF16)

    def weight_grad(late, inner, earlier, current, grads):
        return call(
            functools.partial(weight_grad_kernel, late, inner), [VM] * 3, [VM] * 2, [grad_shape] * 2, []
        )(earlier, current, grads)

    keep_two, send_two = weight_grad(False, 1, hidden_before, hidden, dout)
    grad_two = scatter_grad(keep_two, send_two, core, False)

    dpre = call(
        functools.partial(dpre_kernel, False), [VM] * 3 + [HB] * 4, VM, block(0), scratch
    )(dout, dout_after, slope, *two)
    keep_one, send_one = weight_grad(True, 0, clip_before, clip_ext, dpre)
    grad_one = scatter_grad(keep_one, send_one, core, True)
    return (student, grad_one, grad_two)


def solution(mesh):
    in_specs = (
        P("tm", "height", None, None),
        P("tm", "height", None, None),
        P("height", None),
        P("height", None),
    )
    out_specs = (P("tm", "height", None, None), P("height", None), P("height", None))
    return jax.shard_map(step, mesh=mesh, in_specs=in_specs, out_specs=out_specs, check_vma=False)
```

time: 181 us -> 140 us (0.77)
  Pallas kernels: 44.7 us -> 21.3 us
  waiting for transfers between devices: 80.4 us -> 59.5 us
  starting transfers between devices: 44.6 us -> 52.3 us
  local copies, waits for them, and re-layouts: 6.48 us -> 1.91 us
    pallas_call x5, Pallas kernels: 44.7 us -> 21.3 us  [the longest x2 6.04 us: weight_grad(): call(functools.partial(weight_grad_kernel, late, inner), [VM] * 3, [VM] *...]
    ppermute x16, starting transfers between devices: 22.9 us -> 37.6 us  [stepped(): lax.ppermute(value, BOTH, step_pairs(lax.axis_size('tm'), lax.axis_size('...]
    ppermute x16, waiting for transfers between devices: 64.3 us -> 51.2 us  [stepped(): lax.ppermute(value, BOTH, step_pairs(lax.axis_size('tm'), lax.axis_size('...]
    ppermute x7 -> x5, starting transfers between devices: 19.1 us -> 12.6 us  [shifted(): lax.ppermute(value, axis, [(i, i + by) for i in range(count) if 0 <= i +...]
    ppermute x7 -> x5, waiting for transfers between devices: 11.7 us -> 6.13 us  [shifted(): lax.ppermute(value, axis, [(i, i + by) for i in range(count) if 0 <= i +...]
    unnamed x36 -> x6, local copies, waits for them, and re-layouts: 4.7 us -> 0.94 us
    ppermute x8, waiting for transfers between devices: 4.44 us -> 2.12 us  [swapped(): lax.ppermute(value, 'tm', [(t, t ^ group) for t in range(lax.axis_size('t...]
  transfers between devices with their start and end apart: 31 -> 29, of which waited for: 18 -> 16; matrix products, arithmetic and copies ran while one was open for 2% -> 2% of each run, Pallas kernels for 19% -> 11%
where the time goes in v1:
time: 140 us
  waiting for transfers between devices  59.5 us (42%)
  starting transfers between devices  52.3 us (37%)
  Pallas kernels  21.3 us (15%)
  other arithmetic  3.75 us (3%)
  local copies, waits for them, and re-layouts  1.91 us (1%)
    ppermute x16, waiting for transfers between devices, stepped(): lax.ppermute(value, BOTH, step_pairs(lax.axis_size('tm'), lax.axis_size('...  51.2 us
    ppermute x16, starting transfers between devices, stepped(): lax.ppermute(value, BOTH, step_pairs(lax.axis_size('tm'), lax.axis_size('...  37.6 us
    ppermute x5, starting transfers between devices, shifted(): lax.ppermute(value, axis, [(i, i + by) for i in range(count) if 0 <= i +...  12.6 us
    ppermute x5, waiting for transfers between devices, shifted(): lax.ppermute(value, axis, [(i, i + by) for i in range(count) if 0 <= i +...  6.13 us
    pallas_call x2, Pallas kernels, weight_grad(): call(functools.partial(weight_grad_kernel, late, inner), [VM] * 3, [VM] *...  6.04 us
    pallas_call x1, Pallas kernels, step(): call(functools.partial(conv_one_kernel, True), [VM, VM] + [HB] * 4, [VM,...  5.74 us
    pallas_call x1, Pallas kernels, step(): call(functools.partial(conv_two_kernel, 1.0 / math.sqrt(count_all), False...  5.5 us
    pallas_call x1, Pallas kernels, step(): call(functools.partial(dpre_kernel, False), [VM] * 3 + [HB] * 4, VM, bloc...  4 us
  transfers between devices with their start and end apart: 29, of which 16 were waited for; matrix products, arithmetic and copies ran while one was open for 2% of the time, Pallas kernels for 11%

profile of v1, /device:TPU:0, one launch (start us, length us, event | category | flops | bytes accessed | tf_op | source)
XLA Modules:
  0.0 139.7 jit_solution(4473571790582561953)
XLA Ops:
  1.6 4.1 %collective-permute-start.3 = (bf16[1,432,128]{2,1,0:T(8,128)(2,1)S(1)}, bf16[1,432,128]{2,1,0:T(8,128)(2,1)S(1)}, u32[]{:S(2)}, u32[]{:S(2)}) collective-permute-start(bf16[1,432,128]{2,1,0:T(8,128)(2,1)S(1)} %dynamic-slice_bitcast_fusion.1), channel_id=1, source_target_pairs={{0,8},{1,9},{2,10},{3,11},{4,12},{5,13},{6,14},{7,15},{8,0},{9,1},... | collective-permute-start | bytes 331784 | tf_op jit(solution)/shard_map/ppermute | solution.py:48
  5.7 2.7 %collective-permute-done.3 = bf16[1,432,128]{2,1,0:T(8,128)(2,1)S(1)} collective-permute-done((bf16[1,432,128]{2,1,0:T(8,128)(2,1)S(1)}, bf16[1,432,128]{2,1,0:T(8,128)(2,1)S(1)}, u32[]{:S(2)}, u32[]{:S(2)}) %collective-permute-start.3) | collective-permute-done | bytes 110624 | tf_op jit(solution)/shard_map/ppermute | solution.py:48
  8.5 2.3 %collective-permute-start.4 = (bf16[2,432,128]{2,1,0:T(8,128)(2,1)S(1)}, bf16[2,432,128]{2,1,0:T(8,128)(2,1)S(1)}, u32[]{:S(2)}, u32[]{:S(2)}) collective-permute-start(bf16[2,432,128]{2,1,0:T(8,128)(2,1)S(1)} %pad_maximum_fusion.8), channel_id=1, source_target_pairs={{0,4},{1,5},{2,6},{3,7},{4,0},{5,1},{6,2},{7,3},{8,12},{9,13},{10,... | collective-permute-start | bytes 663560 | tf_op jit(solution)/shard_map/ppermute | solution.py:48
  11.6 1.5 %collective-permute-start.10 = (bf16[1,432,128]{2,1,0:T(8,128)(2,1)S(1)}, bf16[1,432,128]{2,1,0:T(8,128)(2,1)S(1)}, u32[]{:S(2)}, u32[]{:S(2)}) collective-permute-start(bf16[1,432,128]{2,1,0:T(8,128)(2,1)S(1)} %dynamic-slice_bitcast_fusion), channel_id=1, source_target_pairs={{0,1},{1,0},{2,3},{3,2},{4,5},{5,4},{6,7},{7,6},{8,9},{9,8},{10,11... | collective-permute-start | bytes 331784 | tf_op jit(solution)/shard_map/ppermute | solution.py:48
  13.1 2.9 %collective-permute-done.4 = bf16[2,432,128]{2,1,0:T(8,128)(2,1)S(1)} collective-permute-done((bf16[2,432,128]{2,1,0:T(8,128)(2,1)S(1)}, bf16[2,432,128]{2,1,0:T(8,128)(2,1)S(1)}, u32[]{:S(2)}, u32[]{:S(2)}) %collective-permute-start.4) | collective-permute-done | bytes 221216 | tf_op jit(solution)/shard_map/ppermute | solution.py:48
  16.1 1.9 %collective-permute-start.5 = (bf16[4,432,128]{2,1,0:T(8,128)(2,1)S(1)}, bf16[4,432,128]{2,1,0:T(8,128)(2,1)S(1)}, u32[]{:S(2)}, u32[]{:S(2)}) collective-permute-start(bf16[4,432,128]{2,1,0:T(8,128)(2,1)S(1)} %pad_maximum_fusion.4), channel_id=1, source_target_pairs={{0,1},{1,0},{2,3},{3,2},{4,5},{5,4},{6,7},{7,6},{8,9},{9,8},{10,11... | collective-permute-start | bytes 1327112 | tf_op jit(solution)/shard_map/ppermute | solution.py:48
  18.0 2.7 %collective-permute-start.11 = (bf16[2,432,128]{2,1,0:T(8,128)(2,1)S(1)}, bf16[2,432,128]{2,1,0:T(8,128)(2,1)S(1)}, u32[]{:S(2)}, u32[]{:S(2)}) collective-permute-start(bf16[2,432,128]{2,1,0:T(8,128)(2,1)S(1)} %pad_maximum_fusion.9), channel_id=1, source_target_pairs={{0,8},{1,9},{2,10},{3,11},{4,12},{5,13},{6,14},{7,15},{8,0},{9,1},... | collective-permute-start | bytes 663560 | tf_op jit(solution)/shard_map/ppermute | solution.py:48
  20.7 12.0 %collective-permute-done.11 = bf16[2,432,128]{2,1,0:T(8,128)(2,1)S(1)} collective-permute-done((bf16[2,432,128]{2,1,0:T(8,128)(2,1)S(1)}, bf16[2,432,128]{2,1,0:T(8,128)(2,1)S(1)}, u32[]{:S(2)}, u32[]{:S(2)}) %collective-permute-start.11) | collective-permute-done | bytes 221216 | tf_op jit(solution)/shard_map/ppermute | solution.py:48
  32.7 2.4 %collective-permute-start.12 = (bf16[4,432,128]{2,1,0:T(8,128)(2,1)S(1)}, bf16[4,432,128]{2,1,0:T(8,128)(2,1)S(1)}, u32[]{:S(2)}, u32[]{:S(2)}) collective-permute-start(bf16[4,432,128]{2,1,0:T(8,128)(2,1)S(1)} %pad_maximum_fusion.5), channel_id=1, source_target_pairs={{0,4},{1,5},{2,6},{3,7},{4,0},{5,1},{6,2},{7,3},{8,12},{9,13},{10,... | collective-permute-start | bytes 1327112 | tf_op jit(solution)/shard_map/ppermute | solution.py:48
  35.2 1.7 %collective-permute-start.6 = (bf16[8,432,128]{2,1,0:T(8,128)(2,1)S(1)}, bf16[8,432,128]{2,1,0:T(8,128)(2,1)S(1)}, u32[]{:S(2)}, u32[]{:S(2)}) collective-permute-start(bf16[8,432,128]{2,1,0:T(8,128)(2,1)S(1)} %pad_maximum_fusion.near), channel_id=1, source_target_pairs={{0,2},{1,3},{2,0},{3,1},{4,6},{5,7},{6,4},{7,5},{8,10},{9,11},{10,... | collective-permute-start | bytes 2654216 | tf_op jit(solution)/shard_map/ppermute | solution.py:48
  36.9 4.6 %collective-permute-done.12 = bf16[4,432,128]{2,1,0:T(8,128)(2,1)S(1)} collective-permute-done((bf16[4,432,128]{2,1,0:T(8,128)(2,1)S(1)}, bf16[4,432,128]{2,1,0:T(8,128)(2,1)S(1)}, u32[]{:S(2)}, u32[]{:S(2)}) %collective-permute-start.12) | collective-permute-done | bytes 442400 | tf_op jit(solution)/shard_map/ppermute | solution.py:48
  41.6 1.6 %collective-permute-start.13 = (bf16[8,432,128]{2,1,0:T(8,128)(2,1)S(1)}, bf16[8,432,128]{2,1,0:T(8,128)(2,1)S(1)}, u32[]{:S(2)}, u32[]{:S(2)}) collective-permute-start(bf16[8,432,128]{2,1,0:T(8,128)(2,1)S(1)} %pad_maximum_fusion.1.near), channel_id=1, source_target_pairs={{0,2},{1,3},{2,0},{3,1},{4,6},{5,7},{6,4},{7,5},{8,10},{9,11},{10,... | collective-permute-start | bytes 2654216 | tf_op jit(solution)/shard_map/ppermute | solution.py:48
  44.5 4.6 %collective-permute-start = (bf16[2,4,48,256]{3,2,1,0:T(8,128)(2,1)S(1)}, bf16[2,4,48,256]{3,2,1,0:T(8,128)(2,1)S(1)}, u32[]{:S(2)}, u32[]{:S(2)}) collective-permute-start(bf16[2,4,48,256]{3,2,1,0:T(8,128)(2,1)S(1)} %pad_maximum_fusion.10), channel_id=1, source_target_pairs={{0,1},{1,2},{2,3},{3,4},{4,5},{5,6},{6,7},{7,8},{8,9},{9,10},{10,1... | collective-permute-start | bytes 589832 | tf_op jit(solution)/shard_map/ppermute | solution.py:44
  49.7 3.2 %collective-permute-done.1 = bf16[2,4,48,256]{3,2,1,0:T(8,128)(2,1)S(1)} collective-permute-done((bf16[2,4,48,256]{3,2,1,0:T(8,128)(2,1)S(1)}, bf16[2,4,48,256]{3,2,1,0:T(8,128)(2,1)S(1)}, u32[]{:S(2)}, u32[]{:S(2)}) %collective-permute-start.1) | collective-permute-done | bytes 196640 | tf_op jit(solution)/shard_map/ppermute | solution.py:44
  52.9 1.5 %collective-permute-done = bf16[2,4,48,256]{3,2,1,0:T(8,128)(2,1)S(1)} collective-permute-done((bf16[2,4,48,256]{3,2,1,0:T(8,128)(2,1)S(1)}, bf16[2,4,48,256]{3,2,1,0:T(8,128)(2,1)S(1)}, u32[]{:S(2)}, u32[]{:S(2)}) %collective-permute-start) | collective-permute-done | bytes 196640 | tf_op jit(solution)/shard_map/ppermute | solution.py:44
  54.4 2.9 %collective-permute-start.2 = (bf16[2,14,48,256]{3,2,1,0:T(8,128)(2,1)S(1)}, bf16[2,14,48,256]{3,2,1,0:T(8,128)(2,1)S(1)}, u32[]{:S(2)}, u32[]{:S(2)}) collective-permute-start(bf16[2,14,48,256]{3,2,1,0:T(8,128)(2,1)S(1)} %pad_maximum_fusion.2.current.clip), channel_id=1, source_target_pairs={{0,16},{1,17},{2,18},{3,19},{4,20},{5,21},{6,22},{7,23},{8,24},{9,... | collective-permute-start | bytes 2064392 | tf_op jit(solution)/shard_map/ppermute | solution.py:44
  57.4 3.7 %collective-permute-done.13.far = bf16[8,432,128]{2,1,0:T(8,128)(2,1)S(1)} collective-permute-done((bf16[8,432,128]{2,1,0:T(8,128)(2,1)S(1)}, bf16[8,432,128]{2,1,0:T(8,128)(2,1)S(1)}, u32[]{:S(2)}, u32[]{:S(2)}) %collective-permute-start.13) | collective-permute-done | bytes 884768 | tf_op jit(solution)/shard_map/ppermute | solution.py:48
  61.1 5.7 %shard_map.67 = (bf16[2,12,48,256]{3,2,1,0:T(8,128)(2,1)S(1)}, f32[2,8,48,256]{3,2,1,0:T(8,128)S(1)}) custom-call(bf16[2,14,48,256]{3,2,1,0:T(8,128)(2,1)S(1)} %collective-permute-done.2.earlier, bf16[2,14,48,256]{3,2,1,0:T(8,128)(2,1)S(1)} %pad_maximum_fusion.2.current.clip, bf16[8,432,128]{2,1,0:T(8,128)(2,1)S(1)} %pad_maximum_fusion.near, ...), custom_call_target="tpu_custom_call" | custom-call | tf_op jit(solution)/shard_map/pallas_call | solution.py:294
  66.9 2.4 %collective-permute-start.9 = (bf16[2,12,48,256]{3,2,1,0:T(8,128)(2,1)S(1)}, bf16[2,12,48,256]{3,2,1,0:T(8,128)(2,1)S(1)}, u32[]{:S(2)}, u32[]{:S(2)}) collective-permute-start(bf16[2,12,48,256]{3,2,1,0:T(8,128)(2,1)S(1)} %get-tuple-element.11.current), channel_id=1, source_target_pairs={{0,16},{1,17},{2,18},{3,19},{4,20},{5,21},{6,22},{7,23},{8,24},{9,... | collective-permute-start | bytes 1769480 | tf_op jit(solution)/shard_map/ppermute | solution.py:44
  70.9 5.5 %shard_map.68 = (bf16[2,8,48,256]{3,2,1,0:T(8,128)(2,1)}, bf16[2,10,48,256]{3,2,1,0:T(8,128)(2,1)S(1)}) custom-call(bf16[2,12,48,256]{3,2,1,0:T(8,128)(2,1)S(1)} %collective-permute-done.9.earlier, bf16[2,12,48,256]{3,2,1,0:T(8,128)(2,1)S(1)} %get-tuple-element.11.current, bf16[2,14,48,256]{3,2,1,0:T(8,128)(2,1)S(1)} %pad_maximum_fusion.2.current.clip, ...), custom_call_target="tpu_custom_call" | custom-call | tf_op jit(solution)/shard_map/pallas_call | solution.py:300
  77.9 3.0 %shard_map.71 = (bf16[16,432,128]{2,1,0:T(8,128)(2,1)S(1)}, bf16[16,432,128]{2,1,0:T(8,128)(2,1)S(1)}) custom-call(bf16[2,12,48,256]{3,2,1,0:T(8,128)(2,1)S(1)} %collective-permute-done.9.earlier, bf16[2,12,48,256]{3,2,1,0:T(8,128)(2,1)S(1)} %get-tuple-element.11.current, bf16[2,10,48,256]{3,2,1,0:T(8,128)(2,1)S(1)} %get-tuple-element.13.current.grads), custom_call_target="tpu_custom_call" | custom-call | tf_op jit(solution)/shard_map/pallas_call | solution.py:310
  82.1 4.0 %shard_map.69.grads = bf16[2,8,48,256]{3,2,1,0:T(8,128)(2,1)S(1)} custom-call(bf16[2,10,48,256]{3,2,1,0:T(8,128)(2,1)S(1)} %get-tuple-element.13.current.grads, bf16[2,10,48,256]{3,2,1,0:T(8,128)(2,1)S(1)} %collective-permute-done.16.later, f32[2,8,48,256]{3,2,1,0:T(8,128)S(1)} %get-tuple-element.14.slope, bf16[8,432,128]{2,1,0:T(8,128)(2,1)S(1)} %pad_maximum_fusion.1.near, ...), custom_call_target="tpu_custom_call" | custom-call | tf_op jit(solution)/shard_map/pallas_call | solution.py:317
  86.1 3.0 %shard_map.70 = (bf16[16,432,128]{2,1,0:T(8,128)(2,1)S(1)}, bf16[16,432,128]{2,1,0:T(8,128)(2,1)S(1)}) custom-call(bf16[2,14,48,256]{3,2,1,0:T(8,128)(2,1)S(1)} %collective-permute-done.2.earlier, bf16[2,14,48,256]{3,2,1,0:T(8,128)(2,1)S(1)} %pad_maximum_fusion.2.current.clip, bf16[2,8,48,256]{3,2,1,0:T(8,128)(2,1)S(1)} %shard_map.69.grads), custom_call_target="tpu_custom_call" | custom-call | tf_op jit(solution)/shard_map/pallas_call | solution.py:310
  89.7 2.5 %collective-permute-start.24 = (bf16[8,432,128]{2,1,0:T(8,128)(2,1)S(1)}, bf16[8,432,128]{2,1,0:T(8,128)(2,1)S(1)}, u32[]{:S(2)}, u32[]{:S(2)}) collective-permute-start(bf16[8,432,128]{2,1,0:T(8,128)(2,1)S(1)} %get-tuple-element.20), channel_id=1, source_target_pairs={{0,2},{1,3},{2,0},{3,1},{4,6},{5,7},{6,4},{7,5},{8,10},{9,11},{10,... | collective-permute-start | bytes 2654216 | tf_op jit(solution)/shard_map/ppermute | solution.py:48
  93.4 2.5 %collective-permute-start.18 = (bf16[8,432,128]{2,1,0:T(8,128)(2,1)S(1)}, bf16[8,432,128]{2,1,0:T(8,128)(2,1)S(1)}, u32[]{:S(2)}, u32[]{:S(2)}) collective-permute-start(bf16[8,432,128]{2,1,0:T(8,128)(2,1)S(1)} %get-tuple-element.22), channel_id=1, source_target_pairs={{0,2},{1,3},{2,0},{3,1},{4,6},{5,7},{6,4},{7,5},{8,10},{9,11},{10,... | collective-permute-start | bytes 2654216 | tf_op jit(solution)/shard_map/ppermute | solution.py:48
  95.9 7.4 %collective-permute-done.24 = bf16[8,432,128]{2,1,0:T(8,128)(2,1)S(1)} collective-permute-done((bf16[8,432,128]{2,1,0:T(8,128)(2,1)S(1)}, bf16[8,432,128]{2,1,0:T(8,128)(2,1)S(1)}, u32[]{:S(2)}, u32[]{:S(2)}) %collective-permute-start.24) | collective-permute-done | bytes 884768 | tf_op jit(solution)/shard_map/ppermute | solution.py:48
  104.0 8.8 %collective-permute-done.18 = bf16[8,432,128]{2,1,0:T(8,128)(2,1)S(1)} collective-permute-done((bf16[8,432,128]{2,1,0:T(8,128)(2,1)S(1)}, bf16[8,432,128]{2,1,0:T(8,128)(2,1)S(1)}, u32[]{:S(2)}, u32[]{:S(2)}) %collective-permute-start.18) | collective-permute-done | bytes 884768 | tf_op jit(solution)/shard_map/ppermute | solution.py:48
  113.7 3.8 %collective-permute-start.26 = (bf16[2,432,128]{2,1,0:T(8,128)(2,1)S(1)}, bf16[2,432,128]{2,1,0:T(8,128)(2,1)S(1)}, u32[]{:S(2)}, u32[]{:S(2)}) collective-permute-start(bf16[2,432,128]{2,1,0:T(8,128)(2,1)S(1)} %get-tuple-element.27), channel_id=1, source_target_pairs={{0,8},{1,9},{2,10},{3,11},{4,12},{5,13},{6,14},{7,15},{8,0},{9,1},... | collective-permute-start | bytes 663560 | tf_op jit(solution)/shard_map/ppermute | solution.py:48
  117.5 3.8 %collective-permute-done.19 = bf16[4,432,128]{2,1,0:T(8,128)(2,1)S(1)} collective-permute-done((bf16[4,432,128]{2,1,0:T(8,128)(2,1)S(1)}, bf16[4,432,128]{2,1,0:T(8,128)(2,1)S(1)}, u32[]{:S(2)}, u32[]{:S(2)}) %collective-permute-start.19) | collective-permute-done | bytes 442400 | tf_op jit(solution)/shard_map/ppermute | solution.py:48
  122.3 7.3 %collective-permute-start.27 = (bf16[1,432,128]{2,1,0:T(8,128)(2,1)S(1)}, bf16[1,432,128]{2,1,0:T(8,128)(2,1)S(1)}, u32[]{:S(2)}, u32[]{:S(2)}) collective-permute-start(bf16[1,432,128]{2,1,0:T(8,128)(2,1)S(1)} %fusion.2), channel_id=1, source_target_pairs={{0,1},{1,0},{2,3},{3,2},{4,5},{5,4},{6,7},{7,6},{8,9},{9,8},{10,11... | collective-permute-start | bytes 331784 | tf_op jit(solution)/shard_map/ppermute | solution.py:48
  129.6 1.7 %collective-permute-start.21 = (bf16[1,432,128]{2,1,0:T(8,128)(2,1)S(1)}, bf16[1,432,128]{2,1,0:T(8,128)(2,1)S(1)}, u32[]{:S(2)}, u32[]{:S(2)}) collective-permute-start(bf16[1,432,128]{2,1,0:T(8,128)(2,1)S(1)} %fusion.5), channel_id=1, source_target_pairs={{0,8},{1,9},{2,10},{3,11},{4,12},{5,13},{6,14},{7,15},{8,0},{9,1},... | collective-permute-start | bytes 331784 | tf_op jit(solution)/shard_map/ppermute | solution.py:48
  132.4 4.1 %collective-permute-done.21 = bf16[1,432,128]{2,1,0:T(8,128)(2,1)S(1)} collective-permute-done((bf16[1,432,128]{2,1,0:T(8,128)(2,1)S(1)}, bf16[1,432,128]{2,1,0:T(8,128)(2,1)S(1)}, u32[]{:S(2)}, u32[]{:S(2)}) %collective-permute-start.21) | collective-permute-done | bytes 110624 | tf_op jit(solution)/shard_map/ppermute | solution.py:48
  (68 shorter events, 17.1 us)
Async XLA Ops:
  0.6 0.9 copy-start
  1.6 6.9 %collective-permute-start.3 = (bf16[1,432,128]{2,1,0:T(8,128)(2,1)S(1)}, bf16[1,432,128]{2,1,0:T(8,128)(2,1)S(1)}, u32[]{:S(2)}, u32[]{:S(2)}) collective-permute-start(bf16[1,432,128]{2,1,0:T(8,128)(2,1)S(1)} %dynamic-slice_bitcast_fusion.1), channel_id=1, source_target_pairs={{0,8},{1,9},{2,10},{3,11},{4,12},{5,13},{6,14},{7,15},{8,0},{9,1},... | collective-permute-start | bytes 331784 | tf_op jit(solution)/shard_map/ppermute | solution.py:48
  8.5 7.5 %collective-permute-start.4 = (bf16[2,432,128]{2,1,0:T(8,128)(2,1)S(1)}, bf16[2,432,128]{2,1,0:T(8,128)(2,1)S(1)}, u32[]{:S(2)}, u32[]{:S(2)}) collective-permute-start(bf16[2,432,128]{2,1,0:T(8,128)(2,1)S(1)} %pad_maximum_fusion.8), channel_id=1, source_target_pairs={{0,4},{1,5},{2,6},{3,7},{4,0},{5,1},{6,2},{7,3},{8,12},{9,13},{10,... | collective-permute-start | bytes 663560 | tf_op jit(solution)/shard_map/ppermute | solution.py:48
  11.6 6.3 %collective-permute-start.10 = (bf16[1,432,128]{2,1,0:T(8,128)(2,1)S(1)}, bf16[1,432,128]{2,1,0:T(8,128)(2,1)S(1)}, u32[]{:S(2)}, u32[]{:S(2)}) collective-permute-start(bf16[1,432,128]{2,1,0:T(8,128)(2,1)S(1)} %dynamic-slice_bitcast_fusion), channel_id=1, source_target_pairs={{0,1},{1,0},{2,3},{3,2},{4,5},{5,4},{6,7},{7,6},{8,9},{9,8},{10,11... | collective-permute-start | bytes 331784 | tf_op jit(solution)/shard_map/ppermute | solution.py:48
  16.0 20.8 %copy-start.2 = (bf16[2,8,48,256]{3,2,1,0:T(8,128)(2,1)S(1)}, bf16[2,8,48,256]{3,2,1,0:T(8,128)(2,1)}, u32[]{:S(2)}) copy-start(bf16[2,8,48,256]{3,2,1,0:T(8,128)(2,1)} %param.5) | copy-start | bytes 1179652
  16.1 20.8 %copy-start.1 = (bf16[2,8,48,256]{3,2,1,0:T(8,128)(2,1)S(1)}, bf16[2,8,48,256]{3,2,1,0:T(8,128)(2,1)}, u32[]{:S(2)}) copy-start(bf16[2,8,48,256]{3,2,1,0:T(8,128)(2,1)} %param.4) | copy-start | bytes 1179652
  16.1 19.0 %collective-permute-start.5 = (bf16[4,432,128]{2,1,0:T(8,128)(2,1)S(1)}, bf16[4,432,128]{2,1,0:T(8,128)(2,1)S(1)}, u32[]{:S(2)}, u32[]{:S(2)}) collective-permute-start(bf16[4,432,128]{2,1,0:T(8,128)(2,1)S(1)} %pad_maximum_fusion.4), channel_id=1, source_target_pairs={{0,1},{1,0},{2,3},{3,2},{4,5},{5,4},{6,7},{7,6},{8,9},{9,8},{10,11... | collective-permute-start | bytes 1327112 | tf_op jit(solution)/shard_map/ppermute | solution.py:48
  18.0 14.7 %collective-permute-start.11 = (bf16[2,432,128]{2,1,0:T(8,128)(2,1)S(1)}, bf16[2,432,128]{2,1,0:T(8,128)(2,1)S(1)}, u32[]{:S(2)}, u32[]{:S(2)}) collective-permute-start(bf16[2,432,128]{2,1,0:T(8,128)(2,1)S(1)} %pad_maximum_fusion.9), channel_id=1, source_target_pairs={{0,8},{1,9},{2,10},{3,11},{4,12},{5,13},{6,14},{7,15},{8,0},{9,1},... | collective-permute-start | bytes 663560 | tf_op jit(solution)/shard_map/ppermute | solution.py:48
  32.7 8.8 %collective-permute-start.12 = (bf16[4,432,128]{2,1,0:T(8,128)(2,1)S(1)}, bf16[4,432,128]{2,1,0:T(8,128)(2,1)S(1)}, u32[]{:S(2)}, u32[]{:S(2)}) collective-permute-start(bf16[4,432,128]{2,1,0:T(8,128)(2,1)S(1)} %pad_maximum_fusion.5), channel_id=1, source_target_pairs={{0,4},{1,5},{2,6},{3,7},{4,0},{5,1},{6,2},{7,3},{8,12},{9,13},{10,... | collective-permute-start | bytes 1327112 | tf_op jit(solution)/shard_map/ppermute | solution.py:48
  35.2 14.0 %collective-permute-start.6 = (bf16[8,432,128]{2,1,0:T(8,128)(2,1)S(1)}, bf16[8,432,128]{2,1,0:T(8,128)(2,1)S(1)}, u32[]{:S(2)}, u32[]{:S(2)}) collective-permute-start(bf16[8,432,128]{2,1,0:T(8,128)(2,1)S(1)} %pad_maximum_fusion.near), channel_id=1, source_target_pairs={{0,2},{1,3},{2,0},{3,1},{4,6},{5,7},{6,4},{7,5},{8,10},{9,11},{10,... | collective-permute-start | bytes 2654216 | tf_op jit(solution)/shard_map/ppermute | solution.py:48
  41.6 19.5 %collective-permute-start.13 = (bf16[8,432,128]{2,1,0:T(8,128)(2,1)S(1)}, bf16[8,432,128]{2,1,0:T(8,128)(2,1)S(1)}, u32[]{:S(2)}, u32[]{:S(2)}) collective-permute-start(bf16[8,432,128]{2,1,0:T(8,128)(2,1)S(1)} %pad_maximum_fusion.1.near), channel_id=1, source_target_pairs={{0,2},{1,3},{2,0},{3,1},{4,6},{5,7},{6,4},{7,5},{8,10},{9,11},{10,... | collective-permute-start | bytes 2654216 | tf_op jit(solution)/shard_map/ppermute | solution.py:48
  43.2 9.7 %collective-permute-start.1 = (bf16[2,4,48,256]{3,2,1,0:T(8,128)(2,1)S(1)}, bf16[2,4,48,256]{3,2,1,0:T(8,128)(2,1)S(1)}, u32[]{:S(2)}, u32[]{:S(2)}) collective-permute-start(bf16[2,4,48,256]{3,2,1,0:T(8,128)(2,1)S(1)} %pad_maximum_fusion.11), channel_id=1, source_target_pairs={{1,0},{2,1},{3,2},{4,3},{5,4},{6,5},{7,6},{8,7},{9,8},{10,9},{11,1... | collective-permute-start | bytes 589832 | tf_op jit(solution)/shard_map/ppermute | solution.py:44
  44.5 9.8 %collective-permute-start = (bf16[2,4,48,256]{3,2,1,0:T(8,128)(2,1)S(1)}, bf16[2,4,48,256]{3,2,1,0:T(8,128)(2,1)S(1)}, u32[]{:S(2)}, u32[]{:S(2)}) collective-permute-start(bf16[2,4,48,256]{3,2,1,0:T(8,128)(2,1)S(1)} %pad_maximum_fusion.10), channel_id=1, source_target_pairs={{0,1},{1,2},{2,3},{3,4},{4,5},{5,6},{6,7},{7,8},{8,9},{9,10},{10,1... | collective-permute-start | bytes 589832 | tf_op jit(solution)/shard_map/ppermute | solution.py:44
  49.1 12.0 %collective-permute-start.7 = (bf16[8,432,128]{2,1,0:T(8,128)(2,1)S(1)}, bf16[8,432,128]{2,1,0:T(8,128)(2,1)S(1)}, u32[]{:S(2)}, u32[]{:S(2)}) collective-permute-start(bf16[8,432,128]{2,1,0:T(8,128)(2,1)S(1)} %pad_maximum_fusion.near), channel_id=1, source_target_pairs={{0,16},{16,0},{1,17},{17,1},{2,18},{18,2},{3,19},{19,3},{4,20},{20... | collective-permute-start | bytes 2654216 | tf_op jit(solution)/shard_map/ppermute | solution.py:52
  49.2 11.9 %collective-permute-start.8 = (bf16[8,432,128]{2,1,0:T(8,128)(2,1)S(1)}, bf16[8,432,128]{2,1,0:T(8,128)(2,1)S(1)}, u32[]{:S(2)}, u32[]{:S(2)}) collective-permute-start(bf16[8,432,128]{2,1,0:T(8,128)(2,1)S(1)} %collective-permute-done.6.far), channel_id=1, source_target_pairs={{0,16},{16,0},{1,17},{17,1},{2,18},{18,2},{3,19},{19,3},{4,20},{20... | collective-permute-start | bytes 2654216 | tf_op jit(solution)/shard_map/ppermute | solution.py:52
  54.4 6.7 %collective-permute-start.2 = (bf16[2,14,48,256]{3,2,1,0:T(8,128)(2,1)S(1)}, bf16[2,14,48,256]{3,2,1,0:T(8,128)(2,1)S(1)}, u32[]{:S(2)}, u32[]{:S(2)}) collective-permute-start(bf16[2,14,48,256]{3,2,1,0:T(8,128)(2,1)S(1)} %pad_maximum_fusion.2.current.clip), channel_id=1, source_target_pairs={{0,16},{1,17},{2,18},{3,19},{4,20},{5,21},{6,22},{7,23},{8,24},{9,... | collective-permute-start | bytes 2064392 | tf_op jit(solution)/shard_map/ppermute | solution.py:44
  57.3 12.1 %collective-permute-start.14 = (bf16[8,432,128]{2,1,0:T(8,128)(2,1)S(1)}, bf16[8,432,128]{2,1,0:T(8,128)(2,1)S(1)}, u32[]{:S(2)}, u32[]{:S(2)}) collective-permute-start(bf16[8,432,128]{2,1,0:T(8,128)(2,1)S(1)} %pad_maximum_fusion.1.near), channel_id=1, source_target_pairs={{0,16},{16,0},{1,17},{17,1},{2,18},{18,2},{3,19},{19,3},{4,20},{20... | collective-permute-start | bytes 2654216 | tf_op jit(solution)/shard_map/ppermute | solution.py:52
  61.1 8.3 %collective-permute-start.15 = (bf16[8,432,128]{2,1,0:T(8,128)(2,1)S(1)}, bf16[8,432,128]{2,1,0:T(8,128)(2,1)S(1)}, u32[]{:S(2)}, u32[]{:S(2)}) collective-permute-start(bf16[8,432,128]{2,1,0:T(8,128)(2,1)S(1)} %collective-permute-done.13.far), channel_id=1, source_target_pairs={{0,16},{16,0},{1,17},{17,1},{2,18},{18,2},{3,19},{19,3},{4,20},{20... | collective-permute-start | bytes 2654216 | tf_op jit(solution)/shard_map/ppermute | solution.py:52
  66.9 4.0 %collective-permute-start.9 = (bf16[2,12,48,256]{3,2,1,0:T(8,128)(2,1)S(1)}, bf16[2,12,48,256]{3,2,1,0:T(8,128)(2,1)S(1)}, u32[]{:S(2)}, u32[]{:S(2)}) collective-permute-start(bf16[2,12,48,256]{3,2,1,0:T(8,128)(2,1)S(1)} %get-tuple-element.11.current), channel_id=1, source_target_pairs={{0,16},{1,17},{2,18},{3,19},{4,20},{5,21},{6,22},{7,23},{8,24},{9,... | collective-permute-start | bytes 1769480 | tf_op jit(solution)/shard_map/ppermute | solution.py:44
  76.4 5.7 %collective-permute-start.16 = (bf16[2,10,48,256]{3,2,1,0:T(8,128)(2,1)S(1)}, bf16[2,10,48,256]{3,2,1,0:T(8,128)(2,1)S(1)}, u32[]{:S(2)}, u32[]{:S(2)}) collective-permute-start(bf16[2,10,48,256]{3,2,1,0:T(8,128)(2,1)S(1)} %get-tuple-element.13.current.grads), channel_id=1, source_target_pairs={{16,0},{17,1},{18,2},{19,3},{20,4},{21,5},{22,6},{23,7},{24,8},{25... | collective-permute-start | bytes 1474568 | tf_op jit(solution)/shard_map/ppermute | solution.py:44
  80.9 8.3 %collective-permute-start.23 = (bf16[16,432,128]{2,1,0:T(8,128)(2,1)S(1)}, bf16[16,432,128]{2,1,0:T(8,128)(2,1)S(1)}, u32[]{:S(2)}, u32[]{:S(2)}) collective-permute-start(bf16[16,432,128]{2,1,0:T(8,128)(2,1)S(1)} %get-tuple-element.18), channel_id=1, source_target_pairs={{0,16},{16,0},{1,17},{17,1},{2,18},{18,2},{3,19},{19,3},{4,20},{20... | collective-permute-start | bytes 5308424 | tf_op jit(solution)/shard_map/ppermute | solution.py:52
  89.1 3.8 %collective-permute-start.17 = (bf16[16,432,128]{2,1,0:T(8,128)(2,1)S(1)}, bf16[16,432,128]{2,1,0:T(8,128)(2,1)S(1)}, u32[]{:S(2)}, u32[]{:S(2)}) collective-permute-start(bf16[16,432,128]{2,1,0:T(8,128)(2,1)S(1)} %get-tuple-element.16), channel_id=1, source_target_pairs={{0,16},{16,0},{1,17},{17,1},{2,18},{18,2},{3,19},{19,3},{4,20},{20... | collective-permute-start | bytes 5308424 | tf_op jit(solution)/shard_map/ppermute | solution.py:52
  89.7 13.6 %collective-permute-start.24 = (bf16[8,432,128]{2,1,0:T(8,128)(2,1)S(1)}, bf16[8,432,128]{2,1,0:T(8,128)(2,1)S(1)}, u32[]{:S(2)}, u32[]{:S(2)}) collective-permute-start(bf16[8,432,128]{2,1,0:T(8,128)(2,1)S(1)} %get-tuple-element.20), channel_id=1, source_target_pairs={{0,2},{1,3},{2,0},{3,1},{4,6},{5,7},{6,4},{7,5},{8,10},{9,11},{10,... | collective-permute-start | bytes 2654216 | tf_op jit(solution)/shard_map/ppermute | solution.py:48
  93.4 19.4 %collective-permute-start.18 = (bf16[8,432,128]{2,1,0:T(8,128)(2,1)S(1)}, bf16[8,432,128]{2,1,0:T(8,128)(2,1)S(1)}, u32[]{:S(2)}, u32[]{:S(2)}) collective-permute-start(bf16[8,432,128]{2,1,0:T(8,128)(2,1)S(1)} %get-tuple-element.22), channel_id=1, source_target_pairs={{0,2},{1,3},{2,0},{3,1},{4,6},{5,7},{6,4},{7,5},{8,10},{9,11},{10,... | collective-permute-start | bytes 2654216 | tf_op jit(solution)/shard_map/ppermute | solution.py:48
  103.5 10.2 %collective-permute-start.25 = (bf16[4,432,128]{2,1,0:T(8,128)(2,1)S(1)}, bf16[4,432,128]{2,1,0:T(8,128)(2,1)S(1)}, u32[]{:S(2)}, u32[]{:S(2)}) collective-permute-start(bf16[4,432,128]{2,1,0:T(8,128)(2,1)S(1)} %get-tuple-element.23), channel_id=1, source_target_pairs={{0,4},{1,5},{2,6},{3,7},{4,0},{5,1},{6,2},{7,3},{8,12},{9,13},{10,... | collective-permute-start | bytes 1327112 | tf_op jit(solution)/shard_map/ppermute | solution.py:48
  113.0 8.4 %collective-permute-start.19 = (bf16[4,432,128]{2,1,0:T(8,128)(2,1)S(1)}, bf16[4,432,128]{2,1,0:T(8,128)(2,1)S(1)}, u32[]{:S(2)}, u32[]{:S(2)}) collective-permute-start(bf16[4,432,128]{2,1,0:T(8,128)(2,1)S(1)} %get-tuple-element.25), channel_id=1, source_target_pairs={{0,1},{1,0},{2,3},{3,2},{4,5},{5,4},{6,7},{7,6},{8,9},{9,8},{10,11... | collective-permute-start | bytes 1327112 | tf_op jit(solution)/shard_map/ppermute | solution.py:48
  113.7 8.5 %collective-permute-start.26 = (bf16[2,432,128]{2,1,0:T(8,128)(2,1)S(1)}, bf16[2,432,128]{2,1,0:T(8,128)(2,1)S(1)}, u32[]{:S(2)}, u32[]{:S(2)}) collective-permute-start(bf16[2,432,128]{2,1,0:T(8,128)(2,1)S(1)} %get-tuple-element.27), channel_id=1, source_target_pairs={{0,8},{1,9},{2,10},{3,11},{4,12},{5,13},{6,14},{7,15},{8,0},{9,1},... | collective-permute-start | bytes 663560 | tf_op jit(solution)/shard_map/ppermute | solution.py:48
  121.4 8.2 %collective-permute-start.20 = (bf16[2,432,128]{2,1,0:T(8,128)(2,1)S(1)}, bf16[2,432,128]{2,1,0:T(8,128)(2,1)S(1)}, u32[]{:S(2)}, u32[]{:S(2)}) collective-permute-start(bf16[2,432,128]{2,1,0:T(8,128)(2,1)S(1)} %get-tuple-element.29), channel_id=1, source_target_pairs={{0,4},{1,5},{2,6},{3,7},{4,0},{5,1},{6,2},{7,3},{8,12},{9,13},{10,... | collective-permute-start | bytes 663560 | tf_op jit(solution)/shard_map/ppermute | solution.py:48
  122.3 10.0 %collective-permute-start.27 = (bf16[1,432,128]{2,1,0:T(8,128)(2,1)S(1)}, bf16[1,432,128]{2,1,0:T(8,128)(2,1)S(1)}, u32[]{:S(2)}, u32[]{:S(2)}) collective-permute-start(bf16[1,432,128]{2,1,0:T(8,128)(2,1)S(1)} %fusion.2), channel_id=1, source_target_pairs={{0,1},{1,0},{2,3},{3,2},{4,5},{5,4},{6,7},{7,6},{8,9},{9,8},{10,11... | collective-permute-start | bytes 331784 | tf_op jit(solution)/shard_map/ppermute | solution.py:48
  129.6 6.9 %collective-permute-start.21 = (bf16[1,432,128]{2,1,0:T(8,128)(2,1)S(1)}, bf16[1,432,128]{2,1,0:T(8,128)(2,1)S(1)}, u32[]{:S(2)}, u32[]{:S(2)}) collective-permute-start(bf16[1,432,128]{2,1,0:T(8,128)(2,1)S(1)} %fusion.5), channel_id=1, source_target_pairs={{0,8},{1,9},{2,10},{3,11},{4,12},{5,13},{6,14},{7,15},{8,0},{9,1},... | collective-permute-start | bytes 331784 | tf_op jit(solution)/shard_map/ppermute | solution.py:48
  132.3 4.3 %collective-permute-start.28 = (f32[432,128]{1,0:T(8,128)S(1)}, f32[432,128]{1,0:T(8,128)S(1)}, u32[]{:S(2)}, u32[]{:S(2)}) collective-permute-start(f32[432,128]{1,0:T(8,128)S(1)} %fusion.4), channel_id=1, source_target_pairs={{0,16},{16,0},{1,17},{17,1},{2,18},{18,2},{3,19},{19,3},{4,20},{20... | collective-permute-start | bytes 663560 | tf_op jit(solution)/shard_map/ppermute | solution.py:52
  136.6 1.5 %collective-permute-start.22 = (f32[432,128]{1,0:T(8,128)S(1)}, f32[432,128]{1,0:T(8,128)S(1)}, u32[]{:S(2)}, u32[]{:S(2)}) collective-permute-start(f32[432,128]{1,0:T(8,128)S(1)} %fusion.7), channel_id=1, source_target_pairs={{0,16},{16,0},{1,17},{17,1},{2,18},{18,2},{3,19},{19,3},{4,20},{20... | collective-permute-start | bytes 663560 | tf_op jit(solution)/shard_map/ppermute | solution.py:52
